TPU v7x, 256 devices: a whole 4x4x8 slice. The times are simulated.
256 devices in a mesh: replica: 4 (over x_hi, core), fsdp: 64 (over z, y, x_lo).
Axes of the slice: x: 4 (x_hi: 2, x_lo: 2; x = x_hi * 2 + x_lo), y: 4, z: 8, core: 2. Of those that a mesh axis runs over, the one named last changes fastest.
Arguments:
- deltas: bfloat16 [4, 2, 2048, 16384], P('replica', None, 'fsdp'), may hold values from -3 to 3
- master: float32 [2, 2048, 16384], P(None, 'replica', 'fsdp'), may hold values from -3 to 3
- momentum: float32 [2, 2048, 16384], P(None, 'replica', 'fsdp'), may hold values from -2 to 2
Outputs:
- master_out: float32 [2, 2048, 16384], P(None, 'replica', 'fsdp')
- momentum_out: float32 [2, 2048, 16384], P(None, 'replica', 'fsdp')
- params_out: bfloat16 [2, 2048, 16384], P(None, 'fsdp')
All inputs are finite; a program needn't handle non-finite values.
Results may differ from a plain program's by a relative error of at most 0.008.
Values may be sent and summed in bfloat16 or wider, within the bound.
No kernel may reach another device: no remote copies, remote signals or barrier semaphores. Data moves between devices by JAX's collectives and lax.ppermute only.
A program may use at most 64 MiB of HBM per device.

v0:
```python
import jax
import jax.numpy as jnp
import numpy as np
from jax import lax
from jax.experimental import pallas as pl
from jax.experimental.pallas import tpu as pltpu
from jax.sharding import Mesh
from jax.sharding import PartitionSpec as P


AXES = ("xh", "c", "zh", "zm", "z0", "y", "xl")
SIZES = (2, 2, 2, 2, 2, 4, 2)
PLANE = ("zh", "zm", "z0", "y")
REPLICA = ("xh", "c")
FSDP = ("zh", "zm", "z0", "y", "xl")
WIDTH = 256
COLUMNS = 64 * WIDTH
CUT_IN, CUT_OUT = 12, 24
GRANT = 8 << 20


NEAR = pl.BlockSpec(memory_space=pltpu.VMEM)
FAR = pl.BlockSpec(memory_space=pltpu.HBM)


def index(*names):
    total = lax.axis_index(names[0])
    for name in names[1:]:
        total = jnp.bitwise_xor(total, lax.axis_index(name))
    return total


def kept_side():
    return index("xl", "xh", "zh")


def pairs(flip):
    grid = np.arange(np.prod(SIZES)).reshape(SIZES)
    moved = np.flip(grid, [AXES.index(name) for name in flip])
    return [(int(s), int(t)) for s, t in zip(grid.ravel(), moved.ravel(), strict=True)]


def swap(value, *flip):
    return lax.ppermute(value, AXES, pairs(flip))


def exchange(value):
    return lax.all_to_all(value, PLANE, split_axis=0, concat_axis=0, tiled=True)


def on_chip(kernel, operands, outs, far=(), scratch=(), far_outs=(), aliases=None):
    ins = [
        pltpu.with_memory_space_constraint(x, pltpu.HBM if k in far else pltpu.VMEM) for k, x in enumerate(operands)
    ]
    return pl.pallas_call(
        kernel,
        in_specs=[FAR if k in far else NEAR for k in range(len(ins))],
        out_specs=[FAR if k in far_outs else NEAR for k in range(len(outs))],
        out_shape=[
            jax.ShapeDtypeStruct(*out) if k in far_outs else pltpu.VMEM(*out) for k, out in enumerate(outs)
        ],
        scratch_shapes=list(scratch),
        input_output_aliases=aliases or {},
        compiler_params=pltpu.CompilerParams(vmem_limit_bytes=GRANT),
    )(*ins)


def columns_of(ref, proj, k, side):
    return ref.at[proj, :, pl.ds(pl.multiple_of((2 * k + side) * WIDTH, WIDTH), WIDTH)]


def fetch(deltas, other_core, kept, first, count):
    def kernel(src, out, sem):
        proj = 1 - index("c") if other_core else index("c")
        side = kept_side() if kept else 1 - kept_side()

        def start(k, carry):
            pltpu.make_async_copy(columns_of(src, proj, first + k, side), out.at[k], sem).start()
            return carry

        lax.fori_loop(0, count, start, 0, unroll=4)
        pltpu.make_async_copy(out, out, sem).wait()

    out = ((count, deltas.shape[1], WIDTH), deltas.dtype)
    return on_chip(kernel, [deltas], [out], far=(0,), scratch=[pltpu.SemaphoreType.DMA])[0]


def add(*values):
    def kernel(*refs):
        *ins, out = refs

        def body(k, carry):
            total = ins[0][k].astype(jnp.float32)
            for ref in ins[1:]:
                total += ref[k].astype(jnp.float32)
            out[k] = total.astype(out.dtype)
            return carry

        lax.fori_loop(0, out.shape[0], body, 0, unroll=4)

    return on_chip(kernel, values, [(values[0].shape, values[0].dtype)])[0]


def add_kept(mine, theirs, sent):
    def kernel(mine_ref, theirs_ref, *refs):
        *parts, out = refs
        first = 0
        for part in parts:

            def body(k, carry, part=part, first=first):
                total = mine_ref[first + k].astype(jnp.float32) + theirs_ref[first + k].astype(jnp.float32)
                out[first + k] = (total + part[k].astype(jnp.float32)).astype(out.dtype)
                return carry

            lax.fori_loop(0, part.shape[0], body, 0, unroll=4)
            first += part.shape[0]

    return on_chip(kernel, [mine, theirs, *sent], [(mine.shape, mine.dtype)])[0]


def part_rows(spread):
    def kernel(src, over, across, beside):
        xh, c = index("xh"), index("c")
        over[...] = src[1 - xh, c]
        across[...] = src[1 - xh, 1 - c]
        beside[...] = src[xh, 1 - c]

    out = (spread.shape[2:], spread.dtype)
    return on_chip(kernel, [spread], [out, out, out])


def update(spread, over, across, beside, master, momentum):
    count, rows, _ = over.shape

    def kernel(spread_ref, over_ref, across_ref, beside_ref, m_ref, v_ref, mo_ref, vo_ref, *outs):
        xh, c, xl = index("xh"), index("c"), index("xl")
        for p, s, src in ((0, 0, spread_ref.at[xh, c]), (0, 1, over_ref), (1, 0, beside_ref), (1, 1, across_ref)):
            proj, side, dst = jnp.bitwise_xor(c, p), jnp.bitwise_xor(xl, s), outs[2 * p + s]

            def body(k, carry, src=src, dst=dst, proj=proj, side=side):
                at = pl.ds(pl.multiple_of((2 * k + side) * rows, rows), rows)
                outer = src[k].astype(jnp.float32) * 0.25
                velocity = 0.9 * v_ref[proj, at, :] + outer
                updated = m_ref[proj, at, :] - 0.7 * (outer + 0.9 * velocity)
                vo_ref[proj, at, :] = velocity
                mo_ref[proj, at, :] = updated
                dst[k] = updated.astype(dst.dtype)
                return carry

            lax.fori_loop(0, count, body, 0, unroll=2)

    whole, piece = (master.shape, master.dtype), (over.shape, over.dtype)
    operands = [spread, over, across, beside, master, momentum]
    return on_chip(kernel, operands, [whole, whole, piece, piece, piece, piece])


def store(first, second):
    def kernel(first_ref, second_ref, first_out, second_out, sems):
        copies = [
            pltpu.make_async_copy(first_ref, first_out, sems.at[0]),
            pltpu.make_async_copy(second_ref, second_out, sems.at[1]),
        ]
        for copy in copies:
            copy.start()
        for copy in copies:
            copy.wait()

    out = (first.shape, first.dtype)
    return on_chip(kernel, [first, second], [out, out], far_outs=(0, 1), scratch=[pltpu.SemaphoreType.DMA((2,))])


def join_rows(own, over, across, beside):
    def kernel(own_ref, over_ref, across_ref, beside_ref, out):
        xh, c = index("xh"), index("c")
        out[xh, c] = own_ref[...]
        out[1 - xh, c] = over_ref[...]
        out[1 - xh, 1 - c] = across_ref[...]
        out[xh, 1 - c] = beside_ref[...]

    return on_chip(kernel, [own, over, across, beside], [((2, 2, *own.shape), own.dtype)])[0]


def place(pieces, into=None):
    rows = pieces[0][0].shape[1]
    count = len(pieces)

    def kernel(*refs):
        ins, out, sems = refs[:count], refs[-2], refs[-1]
        for j, (src, (_, first, other, kept)) in enumerate(zip(ins, pieces, strict=True)):
            proj = 1 - index("c") if other else index("c")
            side = kept_side() if kept else 1 - kept_side()

            def start(k, carry, j=j, src=src, first=first, proj=proj, side=side):
                pltpu.make_async_copy(src.at[k], columns_of(out, proj, first + k, side), sems.at[j]).start()
                return carry

            lax.fori_loop(0, src.shape[0], start, 0, unroll=4)
        for j, src in enumerate(ins):
            pltpu.make_async_copy(src, src, sems.at[j]).wait()

    operands = [piece[0] for piece in pieces] + ([] if into is None else [into])
    return on_chip(
        kernel,
        operands,
        [((2, rows, COLUMNS), operands[0].dtype)],
        far=(count,),
        far_outs=(0,),
        scratch=[pltpu.SemaphoreType.DMA((count,))],
        aliases=None if into is None else {count: 0},
    )[0]


def on_device(deltas, master, momentum):
    return step(deltas[0], master, momentum)


def across_rows(over, across, beside):
    return swap(over, "xh", "xl"), swap(across, "xh", "xl", "c"), swap(beside, "c")


def step(local, master, momentum):
    blocks = local.shape[2] // (2 * WIDTH)
    sent = []
    for first, count in ((0, CUT_IN), (CUT_IN, blocks - CUT_IN)):
        theirs = swap(fetch(local, True, False, first, count), "c")
        sent.append(swap(add(fetch(local, False, False, first, count), theirs), "xh"))
    theirs = swap(fetch(local, True, True, 0, blocks), "c")
    mine = fetch(local, False, True, 0, blocks)
    summed = add_kept(mine, theirs, sent)

    spread = exchange(summed)
    spread = spread.reshape(2, 2, -1, *spread.shape[1:])
    moved = across_rows(*part_rows(spread))
    updated, velocity, own, over, beside, across = update(spread, *moved, master, momentum)

    moved = across_rows(over, across, beside)
    kept = exchange(join_rows(own, *moved).reshape(summed.shape))
    early, late = swap(kept[:CUT_OUT], "xh"), swap(kept[CUT_OUT:], "xh")
    pieces = [(kept, 0, False, True), (swap(kept, "c"), 0, True, True)]
    params = place(pieces)
    updated, velocity = store(updated, velocity)
    early, params, updated, velocity = lax.optimization_barrier((early, params, updated, velocity))
    params = place([(early, 0, False, False), (swap(early, "c"), 0, True, False)], params)
    params = place([(late, CUT_OUT, False, False), (swap(late, "c"), CUT_OUT, True, False)], params)
    return updated, velocity, params


def solution(mesh):
    parts = Mesh(mesh.devices.reshape(SIZES), AXES)
    return jax.shard_map(
        on_device,
        mesh=parts,
        in_specs=(P(REPLICA, None, FSDP, None), P(None, REPLICA, FSDP), P(None, REPLICA, FSDP)),
        out_specs=(P(None, REPLICA, FSDP), P(None, REPLICA, FSDP), P(None, FSDP, None)),
        check_vma=False,
    )
```

profile of v0, /device:TPU:1, one launch (start us, length us, event | category | flops | bytes accessed | tf_op | source)
XLA Modules:
  0.0 115.1 jit_solution(4845734468715526953)
XLA Ops:
  0.6 1.0 shard_map.64
  1.6 3.3 %collective-permute-start.3 = (bf16[20,32,256]{2,1,0:T(8,128)(2,1)S(1)}, bf16[20,32,256]{2,1,0:T(8,128)(2,1)S(1)}, u32[]{:S(2)}, u32[]{:S(2)}) collective-permute-start(bf16[20,32,256]{2,1,0:T(8,128)(2,1)S(1)} %shard_map.64), channel_id=1, source_target_pairs={{0,64},{1,65},{2,66},{3,67},{4,68},{5,69},{6,70},{7,71},{8,72},{9,... | collective-permute-start | bytes 983048 | tf_op jit(solution)/shard_map/ppermute | solution.py:44
  4.9 1.0 shard_map.59
  5.9 0.1 collective-permute-start
  6.0 0.9 shard_map.61
  6.9 0.5 collective-permute-start.1
  7.5 0.9 shard_map.63.refs_0_
  8.4 0.0 collective-permute-done.3.refs_1_
  8.4 0.1 shard_map.65
  8.5 1.1 collective-permute-start.4
  9.7 0.9 shard_map.60.refs_0_
  10.5 0.0 collective-permute-done.1.refs_1_
  10.5 0.1 shard_map.62
  10.6 2.0 %collective-permute-start.2 = (bf16[12,32,256]{2,1,0:T(8,128)(2,1)S(1)}, bf16[12,32,256]{2,1,0:T(8,128)(2,1)S(1)}, u32[]{:S(2)}, u32[]{:S(2)}) collective-permute-start(bf16[12,32,256]{2,1,0:T(8,128)(2,1)S(1)} %shard_map.62), channel_id=1, source_target_pairs={{0,128},{1,129},{2,130},{3,131},{4,132},{5,133},{6,134},{7,135},{8... | collective-permute-start | bytes 589832 | tf_op jit(solution)/shard_map/ppermute | solution.py:44
  12.6 1.0 shard_map.58.mine_ref
  13.6 0.0 copy-start
  13.7 0.0 copy-start.1
  13.7 9.9 %collective-permute-done.2.refs_0_ = bf16[12,32,256]{2,1,0:T(8,128)(2,1)S(1)} collective-permute-done((bf16[12,32,256]{2,1,0:T(8,128)(2,1)S(1)}, bf16[12,32,256]{2,1,0:T(8,128)(2,1)S(1)}, u32[]{:S(2)}, u32[]{:S(2)}) %collective-permute-start.2) | collective-permute-done | bytes 196640 | tf_op jit(solution)/shard_map/ppermute | solution.py:44
  23.5 0.0 collective-permute-done.theirs_ref
  23.5 0.0 collective-permute-done.4.refs_1_
  23.5 0.2 shard_map.66
  23.8 24.7 %all_to_all.10 = bf16[32,32,256]{2,1,0:T(8,128)(2,1)S(1)} all-to-all(bf16[32,32,256]{2,1,0:T(8,128)(2,1)S(1)} %shard_map.66), channel_id=1, replica_groups=mesh['xh'=2,'c'=2,'zh'=2,'zm'=2,'z0'=2,'y'=4,'xl'=2] {'zh','zm','z0','y'}, dimensions={0} | all-to-all | bytes 1048576 | tf_op jit(solution)/shard_map/all_to_all | solution.py:48
  48.5 2.6 %collective-permute-start.5 = (bf16[8,32,256]{2,1,0:T(8,128)(2,1)S(1)}, bf16[8,32,256]{2,1,0:T(8,128)(2,1)S(1)}, u32[]{:S(2)}, u32[]{:S(2)}) collective-permute-start(bf16[8,32,256]{2,1,0:T(8,128)(2,1)S(1)} %get-tuple-element.18), channel_id=1, source_target_pairs={{0,129},{1,128},{2,131},{3,130},{4,133},{5,132},{6,135},{7,134},{8... | collective-permute-start | bytes 393224 | tf_op jit(solution)/shard_map/ppermute | solution.py:44
  51.1 3.6 %collective-permute-start.6 = (bf16[8,32,256]{2,1,0:T(8,128)(2,1)S(1)}, bf16[8,32,256]{2,1,0:T(8,128)(2,1)S(1)}, u32[]{:S(2)}, u32[]{:S(2)}) collective-permute-start(bf16[8,32,256]{2,1,0:T(8,128)(2,1)S(1)} %get-tuple-element.19), channel_id=1, source_target_pairs={{0,193},{1,192},{2,195},{3,194},{4,197},{5,196},{6,199},{7,198},{8... | collective-permute-start | bytes 393224 | tf_op jit(solution)/shard_map/ppermute | solution.py:44
  54.7 0.0 collective-permute-start.7
  54.7 0.0 collective-permute-done.5.over_ref
  54.7 5.0 %collective-permute-done.6.across_ref = bf16[8,32,256]{2,1,0:T(8,128)(2,1)S(1)} collective-permute-done((bf16[8,32,256]{2,1,0:T(8,128)(2,1)S(1)}, bf16[8,32,256]{2,1,0:T(8,128)(2,1)S(1)}, u32[]{:S(2)}, u32[]{:S(2)}) %collective-permute-start.6) | collective-permute-done | bytes 131104 | tf_op jit(solution)/shard_map/ppermute | solution.py:44
  59.7 0.0 collective-permute-done.7.beside_ref
  59.7 0.4 shard_map.68
  60.2 3.0 %collective-permute-start.8 = (bf16[8,32,256]{2,1,0:T(8,128)(2,1)S(1)}, bf16[8,32,256]{2,1,0:T(8,128)(2,1)S(1)}, u32[]{:S(2)}, u32[]{:S(2)}) collective-permute-start(bf16[8,32,256]{2,1,0:T(8,128)(2,1)S(1)} %get-tuple-element.22), channel_id=1, source_target_pairs={{0,129},{1,128},{2,131},{3,130},{4,133},{5,132},{6,135},{7,134},{8... | collective-permute-start | bytes 393224 | tf_op jit(solution)/shard_map/ppermute | solution.py:44
  63.1 1.1 collective-permute-start.9
  64.3 2.2 %collective-permute-done.8.over_ref = bf16[8,32,256]{2,1,0:T(8,128)(2,1)S(1)} collective-permute-done((bf16[8,32,256]{2,1,0:T(8,128)(2,1)S(1)}, bf16[8,32,256]{2,1,0:T(8,128)(2,1)S(1)}, u32[]{:S(2)}, u32[]{:S(2)}) %collective-permute-start.8) | collective-permute-done | bytes 131104 | tf_op jit(solution)/shard_map/ppermute | solution.py:44
  66.4 3.3 %collective-permute-done.9.across_ref = bf16[8,32,256]{2,1,0:T(8,128)(2,1)S(1)} collective-permute-done((bf16[8,32,256]{2,1,0:T(8,128)(2,1)S(1)}, bf16[8,32,256]{2,1,0:T(8,128)(2,1)S(1)}, u32[]{:S(2)}, u32[]{:S(2)}) %collective-permute-start.9) | collective-permute-done | bytes 131104 | tf_op jit(solution)/shard_map/ppermute | solution.py:44
  69.7 0.0 collective-permute-done.10.beside_ref
  69.8 20.9 %all_to_all.11.refs_0_ = bf16[32,32,256]{2,1,0:T(8,128)(2,1)S(1)} all-to-all(bf16[32,32,256]{2,1,0:T(8,128)(2,1)S(1)} %bitcast.5), channel_id=1, replica_groups=mesh['xh'=2,'c'=2,'zh'=2,'zm'=2,'z0'=2,'y'=4,'xl'=2] {'zh','zm','z0','y'}, dimensions={0} | all-to-all | bytes 1048576 | tf_op jit(solution)/shard_map/all_to_all | solution.py:48
  90.7 2.1 %collective-permute-start.12 = (bf16[32,32,256]{2,1,0:T(8,128)(2,1)S(1)}, bf16[32,32,256]{2,1,0:T(8,128)(2,1)S(1)}, u32[]{:S(2)}, u32[]{:S(2)}) collective-permute-start(bf16[32,32,256]{2,1,0:T(8,128)(2,1)S(1)} %all_to_all.11.refs_0_), channel_id=1, source_target_pairs={{0,64},{1,65},{2,66},{3,67},{4,68},{5,69},{6,70},{7,71},{8,72},{9,... | collective-permute-start | bytes 1572872 | tf_op jit(solution)/shard_map/ppermute | solution.py:44
  92.8 0.4 collective-permute-start.11
  93.1 1.3 %shard_map.71 = (f32[2,512,256]{2,1,0:T(8,128)}, f32[2,512,256]{2,1,0:T(8,128)}) custom-call(f32[2,512,256]{2,1,0:T(8,128)S(1)} %get-tuple-element.25.first_ref, f32[2,512,256]{2,1,0:T(8,128)S(1)} %get-tuple-element.26.second_ref), custom_call_target="tpu_custom_call" | custom-call | tf_op jit(solution)/shard_map/pallas_call | solution.py:55
  94.5 0.0 collective-permute-done.12.refs_1_
  94.5 1.0 shard_map.70.refs_2_
  95.5 9.6 %collective-permute-done.11.refs_0_ = bf16[24,32,256]{2,1,0:T(8,128)(2,1)S(1)} collective-permute-done((bf16[24,32,256]{2,1,0:T(8,128)(2,1)S(1)}, bf16[24,32,256]{2,1,0:T(8,128)(2,1)S(1)}, u32[]{:S(2)}, u32[]{:S(2)}) %collective-permute-start.11) | collective-permute-done | bytes 393248 | tf_op jit(solution)/shard_map/ppermute | solution.py:44
  105.0 0.9 collective-permute-start.15
  105.9 0.4 collective-permute-start.13
  106.3 6.3 %collective-permute-done.13.refs_0_ = bf16[8,32,256]{2,1,0:T(8,128)(2,1)S(1)} collective-permute-done((bf16[8,32,256]{2,1,0:T(8,128)(2,1)S(1)}, bf16[8,32,256]{2,1,0:T(8,128)(2,1)S(1)}, u32[]{:S(2)}, u32[]{:S(2)}) %collective-permute-start.13) | collective-permute-done | bytes 131104 | tf_op jit(solution)/shard_map/ppermute | solution.py:44
  112.5 0.9 collective-permute-start.14
  113.4 0.9 shard_map.72.refs_2_
  114.3 0.1 collective-permute-done.14.refs_1_
  114.4 0.7 shard_map.73
  (8 shorter events, 0.1 us)
Async XLA Ops:
  1.6 6.8 %collective-permute-start.3 = (bf16[20,32,256]{2,1,0:T(8,128)(2,1)S(1)}, bf16[20,32,256]{2,1,0:T(8,128)(2,1)S(1)}, u32[]{:S(2)}, u32[]{:S(2)}) collective-permute-start(bf16[20,32,256]{2,1,0:T(8,128)(2,1)S(1)} %shard_map.64), channel_id=1, source_target_pairs={{0,64},{1,65},{2,66},{3,67},{4,68},{5,69},{6,70},{7,71},{8,72},{9,... | collective-permute-start | bytes 983048 | tf_op jit(solution)/shard_map/ppermute | solution.py:44
  5.9 17.6 %collective-permute-start = (bf16[32,32,256]{2,1,0:T(8,128)(2,1)S(1)}, bf16[32,32,256]{2,1,0:T(8,128)(2,1)S(1)}, u32[]{:S(2)}, u32[]{:S(2)}) collective-permute-start(bf16[32,32,256]{2,1,0:T(8,128)(2,1)S(1)} %shard_map.59), channel_id=1, source_target_pairs={{0,64},{1,65},{2,66},{3,67},{4,68},{5,69},{6,70},{7,71},{8,72},{9,... | collective-permute-start | bytes 1572872 | tf_op jit(solution)/shard_map/ppermute | solution.py:44
  6.9 3.6 %collective-permute-start.1 = (bf16[12,32,256]{2,1,0:T(8,128)(2,1)S(1)}, bf16[12,32,256]{2,1,0:T(8,128)(2,1)S(1)}, u32[]{:S(2)}, u32[]{:S(2)}) collective-permute-start(bf16[12,32,256]{2,1,0:T(8,128)(2,1)S(1)} %shard_map.61), channel_id=1, source_target_pairs={{0,64},{1,65},{2,66},{3,67},{4,68},{5,69},{6,70},{7,71},{8,72},{9,... | collective-permute-start | bytes 589832 | tf_op jit(solution)/shard_map/ppermute | solution.py:44
  8.5 15.0 %collective-permute-start.4 = (bf16[20,32,256]{2,1,0:T(8,128)(2,1)S(1)}, bf16[20,32,256]{2,1,0:T(8,128)(2,1)S(1)}, u32[]{:S(2)}, u32[]{:S(2)}) collective-permute-start(bf16[20,32,256]{2,1,0:T(8,128)(2,1)S(1)} %shard_map.65), channel_id=1, source_target_pairs={{0,128},{1,129},{2,130},{3,131},{4,132},{5,133},{6,134},{7,135},{8... | collective-permute-start | bytes 983048 | tf_op jit(solution)/shard_map/ppermute | solution.py:44
  10.6 12.9 %collective-permute-start.2 = (bf16[12,32,256]{2,1,0:T(8,128)(2,1)S(1)}, bf16[12,32,256]{2,1,0:T(8,128)(2,1)S(1)}, u32[]{:S(2)}, u32[]{:S(2)}) collective-permute-start(bf16[12,32,256]{2,1,0:T(8,128)(2,1)S(1)} %shard_map.62), channel_id=1, source_target_pairs={{0,128},{1,129},{2,130},{3,131},{4,132},{5,133},{6,134},{7,135},{8... | collective-permute-start | bytes 589832 | tf_op jit(solution)/shard_map/ppermute | solution.py:44
  13.6 46.1 %copy-start = (f32[2,512,256]{2,1,0:T(8,128)S(1)}, f32[2,512,256]{2,1,0:T(8,128)}, u32[]{:S(2)}) copy-start(f32[2,512,256]{2,1,0:T(8,128)} %m_ref.1) | copy-start | bytes 3145732
  13.7 46.1 %copy-start.1 = (f32[2,512,256]{2,1,0:T(8,128)S(1)}, f32[2,512,256]{2,1,0:T(8,128)}, u32[]{:S(2)}) copy-start(f32[2,512,256]{2,1,0:T(8,128)} %v_ref.1) | copy-start | bytes 3145732
  48.5 6.2 %collective-permute-start.5 = (bf16[8,32,256]{2,1,0:T(8,128)(2,1)S(1)}, bf16[8,32,256]{2,1,0:T(8,128)(2,1)S(1)}, u32[]{:S(2)}, u32[]{:S(2)}) collective-permute-start(bf16[8,32,256]{2,1,0:T(8,128)(2,1)S(1)} %get-tuple-element.18), channel_id=1, source_target_pairs={{0,129},{1,128},{2,131},{3,130},{4,133},{5,132},{6,135},{7,134},{8... | collective-permute-start | bytes 393224 | tf_op jit(solution)/shard_map/ppermute | solution.py:44
  51.1 8.6 %collective-permute-start.6 = (bf16[8,32,256]{2,1,0:T(8,128)(2,1)S(1)}, bf16[8,32,256]{2,1,0:T(8,128)(2,1)S(1)}, u32[]{:S(2)}, u32[]{:S(2)}) collective-permute-start(bf16[8,32,256]{2,1,0:T(8,128)(2,1)S(1)} %get-tuple-element.19), channel_id=1, source_target_pairs={{0,193},{1,192},{2,195},{3,194},{4,197},{5,196},{6,199},{7,198},{8... | collective-permute-start | bytes 393224 | tf_op jit(solution)/shard_map/ppermute | solution.py:44
  54.7 5.0 %collective-permute-start.7 = (bf16[8,32,256]{2,1,0:T(8,128)(2,1)S(1)}, bf16[8,32,256]{2,1,0:T(8,128)(2,1)S(1)}, u32[]{:S(2)}, u32[]{:S(2)}) collective-permute-start(bf16[8,32,256]{2,1,0:T(8,128)(2,1)S(1)} %get-tuple-element.20), channel_id=1, source_target_pairs={{0,64},{1,65},{2,66},{3,67},{4,68},{5,69},{6,70},{7,71},{8,72},{9,... | collective-permute-start | bytes 393224 | tf_op jit(solution)/shard_map/ppermute | solution.py:44
  60.2 6.3 %collective-permute-start.8 = (bf16[8,32,256]{2,1,0:T(8,128)(2,1)S(1)}, bf16[8,32,256]{2,1,0:T(8,128)(2,1)S(1)}, u32[]{:S(2)}, u32[]{:S(2)}) collective-permute-start(bf16[8,32,256]{2,1,0:T(8,128)(2,1)S(1)} %get-tuple-element.22), channel_id=1, source_target_pairs={{0,129},{1,128},{2,131},{3,130},{4,133},{5,132},{6,135},{7,134},{8... | collective-permute-start | bytes 393224 | tf_op jit(solution)/shard_map/ppermute | solution.py:44
  63.1 6.6 %collective-permute-start.9 = (bf16[8,32,256]{2,1,0:T(8,128)(2,1)S(1)}, bf16[8,32,256]{2,1,0:T(8,128)(2,1)S(1)}, u32[]{:S(2)}, u32[]{:S(2)}) collective-permute-start(bf16[8,32,256]{2,1,0:T(8,128)(2,1)S(1)} %get-tuple-element.23), channel_id=1, source_target_pairs={{0,193},{1,192},{2,195},{3,194},{4,197},{5,196},{6,199},{7,198},{8... | collective-permute-start | bytes 393224 | tf_op jit(solution)/shard_map/ppermute | solution.py:44
  64.3 5.5 %collective-permute-start.10 = (bf16[8,32,256]{2,1,0:T(8,128)(2,1)S(1)}, bf16[8,32,256]{2,1,0:T(8,128)(2,1)S(1)}, u32[]{:S(2)}, u32[]{:S(2)}) collective-permute-start(bf16[8,32,256]{2,1,0:T(8,128)(2,1)S(1)} %get-tuple-element.24), channel_id=1, source_target_pairs={{0,64},{1,65},{2,66},{3,67},{4,68},{5,69},{6,70},{7,71},{8,72},{9,... | collective-permute-start | bytes 393224 | tf_op jit(solution)/shard_map/ppermute | solution.py:44
  90.7 3.8 %collective-permute-start.12 = (bf16[32,32,256]{2,1,0:T(8,128)(2,1)S(1)}, bf16[32,32,256]{2,1,0:T(8,128)(2,1)S(1)}, u32[]{:S(2)}, u32[]{:S(2)}) collective-permute-start(bf16[32,32,256]{2,1,0:T(8,128)(2,1)S(1)} %all_to_all.11.refs_0_), channel_id=1, source_target_pairs={{0,64},{1,65},{2,66},{3,67},{4,68},{5,69},{6,70},{7,71},{8,72},{9,... | collective-permute-start | bytes 1572872 | tf_op jit(solution)/shard_map/ppermute | solution.py:44
  92.8 12.3 %collective-permute-start.11 = (bf16[24,32,256]{2,1,0:T(8,128)(2,1)S(1)}, bf16[24,32,256]{2,1,0:T(8,128)(2,1)S(1)}, u32[]{:S(2)}, u32[]{:S(2)}) collective-permute-start(bf16[24,32,256]{2,1,0:T(8,128)(2,1)S(1)} %slice.8), channel_id=1, source_target_pairs={{0,128},{1,129},{2,130},{3,131},{4,132},{5,133},{6,134},{7,135},{8... | collective-permute-start | bytes 1179656 | tf_op jit(solution)/shard_map/ppermute | solution.py:44
  105.0 8.4 %collective-permute-start.15 = (bf16[24,32,256]{2,1,0:T(8,128)(2,1)S(1)}, bf16[24,32,256]{2,1,0:T(8,128)(2,1)S(1)}, u32[]{:S(2)}, u32[]{:S(2)}) collective-permute-start(bf16[24,32,256]{2,1,0:T(8,128)(2,1)S(1)} %collective-permute-done.11.refs_0_), channel_id=1, source_target_pairs={{0,64},{1,65},{2,66},{3,67},{4,68},{5,69},{6,70},{7,71},{8,72},{9,... | collective-permute-start | bytes 1179656 | tf_op jit(solution)/shard_map/ppermute | solution.py:44
  105.9 6.6 %collective-permute-start.13 = (bf16[8,32,256]{2,1,0:T(8,128)(2,1)S(1)}, bf16[8,32,256]{2,1,0:T(8,128)(2,1)S(1)}, u32[]{:S(2)}, u32[]{:S(2)}) collective-permute-start(bf16[8,32,256]{2,1,0:T(8,128)(2,1)S(1)} %slice.9), channel_id=1, source_target_pairs={{0,128},{1,129},{2,130},{3,131},{4,132},{5,133},{6,134},{7,135},{8... | collective-permute-start | bytes 393224 | tf_op jit(solution)/shard_map/ppermute | solution.py:44
  112.5 1.8 %collective-permute-start.14 = (bf16[8,32,256]{2,1,0:T(8,128)(2,1)S(1)}, bf16[8,32,256]{2,1,0:T(8,128)(2,1)S(1)}, u32[]{:S(2)}, u32[]{:S(2)}) collective-permute-start(bf16[8,32,256]{2,1,0:T(8,128)(2,1)S(1)} %collective-permute-done.13.refs_0_), channel_id=1, source_target_pairs={{0,64},{1,65},{2,66},{3,67},{4,68},{5,69},{6,70},{7,71},{8,72},{9,... | collective-permute-start | bytes 393224 | tf_op jit(solution)/shard_map/ppermute | solution.py:44
where the time goes:
time: 116 us; the launch traced here: 115 us
  blocking collectives  45.6 us (39%)
  waiting for transfers between devices  36.2 us (31%)
  starting transfers between devices  21.9 us (19%)
  Pallas kernels  10.4 us (9%)
    all_to_all x2, blocking collectives, exchange(): return lax.all_to_all(value, PLANE, split_axis=0, concat_axis=0, tiled=True)  45.6 us
    ppermute x16, waiting for transfers between devices, swap(): return lax.ppermute(value, AXES, pairs(flip))  36.2 us
    ppermute x16, starting transfers between devices, swap(): return lax.ppermute(value, AXES, pairs(flip))  21.9 us
    pallas_call x16, Pallas kernels, on_chip(): pl.pallas_call(kernel, in_specs=[FAR if k in far else NEAR for k in range...  10.4 us
  transfers between devices with their start and end apart: 16, of which 7 were waited for; matrix products, arithmetic and copies ran while one was open for 0% of the time, Pallas kernels for 7%

commit v1 on v0

--- a/solution.py
+++ b/solution.py
@@ -15,7 +15,7 @@
 FSDP = ("zh", "zm", "z0", "y", "xl")
 WIDTH = 256
 COLUMNS = 64 * WIDTH
-CUT_IN, CUT_OUT = 12, 24
+CUT = 24
 GRANT = 8 << 20
 
 
@@ -44,8 +44,8 @@
     return lax.ppermute(value, AXES, pairs(flip))
 
 
-def exchange(value):
-    return lax.all_to_all(value, PLANE, split_axis=0, concat_axis=0, tiled=True)
+def exchange(value, axes):
+    return lax.all_to_all(value, axes, split_axis=0, concat_axis=0, tiled=True)
 
 
 def on_chip(kernel, operands, outs, far=(), scratch=(), far_outs=(), aliases=None):
@@ -65,17 +65,18 @@
     )(*ins)
 
 
-def columns_of(ref, proj, k, side):
-    return ref.at[proj, :, pl.ds(pl.multiple_of((2 * k + side) * WIDTH, WIDTH), WIDTH)]
-
-
-def fetch(deltas, other_core, kept, first, count):
+def columns_of(ref, proj, block):
+    return ref.at[proj, :, pl.ds(pl.multiple_of(block * WIDTH, WIDTH), WIDTH)]
+
+
+def fetch(deltas, other_core):
+    count = deltas.shape[2] // WIDTH
+
     def kernel(src, out, sem):
         proj = 1 - index("c") if other_core else index("c")
-        side = kept_side() if kept else 1 - kept_side()
 
         def start(k, carry):
-            pltpu.make_async_copy(columns_of(src, proj, first + k, side), out.at[k], sem).start()
+            pltpu.make_async_copy(columns_of(src, proj, k), out.at[k], sem).start()
             return carry
 
         lax.fori_loop(0, count, start, 0, unroll=4)
@@ -101,56 +102,42 @@
     return on_chip(kernel, values, [(values[0].shape, values[0].dtype)])[0]
 
 
-def add_kept(mine, theirs, sent):
-    def kernel(mine_ref, theirs_ref, *refs):
-        *parts, out = refs
-        first = 0
-        for part in parts:
-
-            def body(k, carry, part=part, first=first):
-                total = mine_ref[first + k].astype(jnp.float32) + theirs_ref[first + k].astype(jnp.float32)
-                out[first + k] = (total + part[k].astype(jnp.float32)).astype(out.dtype)
-                return carry
-
-            lax.fori_loop(0, part.shape[0], body, 0, unroll=4)
-            first += part.shape[0]
-
-    return on_chip(kernel, [mine, theirs, *sent], [(mine.shape, mine.dtype)])[0]
-
-
 def part_rows(spread):
-    def kernel(src, over, across, beside):
+    def kernel(src, over, beside_other, beside_own):
         xh, c = index("xh"), index("c")
         over[...] = src[1 - xh, c]
-        across[...] = src[1 - xh, 1 - c]
-        beside[...] = src[xh, 1 - c]
+        beside_other[...] = src[1 - xh, 1 - c]
+        beside_own[...] = src[xh, 1 - c]
 
     out = (spread.shape[2:], spread.dtype)
     return on_chip(kernel, [spread], [out, out, out])
 
 
-def update(spread, over, across, beside, master, momentum):
-    count, rows, _ = over.shape
-
-    def kernel(spread_ref, over_ref, across_ref, beside_ref, m_ref, v_ref, mo_ref, vo_ref, *outs):
+def update(spread, over, beside, across, master, momentum):
+    blocks, rows, _ = over.shape
+
+    def kernel(spread_ref, over_ref, beside_ref, across_ref, m_ref, v_ref, mo_ref, vo_ref, *outs):
         xh, c, xl = index("xh"), index("c"), index("xl")
-        for p, s, src in ((0, 0, spread_ref.at[xh, c]), (0, 1, over_ref), (1, 0, beside_ref), (1, 1, across_ref)):
-            proj, side, dst = jnp.bitwise_xor(c, p), jnp.bitwise_xor(xl, s), outs[2 * p + s]
-
-            def body(k, carry, src=src, dst=dst, proj=proj, side=side):
-                at = pl.ds(pl.multiple_of((2 * k + side) * rows, rows), rows)
-                outer = src[k].astype(jnp.float32) * 0.25
-                velocity = 0.9 * v_ref[proj, at, :] + outer
-                updated = m_ref[proj, at, :] - 0.7 * (outer + 0.9 * velocity)
-                vo_ref[proj, at, :] = velocity
-                mo_ref[proj, at, :] = updated
-                dst[k] = updated.astype(dst.dtype)
-                return carry
-
-            lax.fori_loop(0, count, body, 0, unroll=2)
-
-    whole, piece = (master.shape, master.dtype), (over.shape, over.dtype)
-    operands = [spread, over, across, beside, master, momentum]
+        for p, here, there in ((0, spread_ref.at[xh, c], over_ref), (1, beside_ref, across_ref)):
+            proj = jnp.bitwise_xor(c, p)
+            for s in range(2):
+                side, dst = jnp.bitwise_xor(xl, s), outs[2 * p + s]
+
+                def body(k, carry, here=here, there=there, dst=dst, proj=proj, side=side):
+                    block = 2 * k + side
+                    at = pl.ds(pl.multiple_of(block * rows, rows), rows)
+                    outer = (here[block].astype(jnp.float32) + there[block].astype(jnp.float32)) * 0.25
+                    velocity = 0.9 * v_ref[proj, at, :] + outer
+                    updated = m_ref[proj, at, :] - 0.7 * (outer + 0.9 * velocity)
+                    vo_ref[proj, at, :] = velocity
+                    mo_ref[proj, at, :] = updated
+                    dst[k] = updated.astype(dst.dtype)
+                    return carry
+
+                lax.fori_loop(0, blocks // 2, body, 0, unroll=2)
+
+    whole, piece = (master.shape, master.dtype), ((blocks // 2, *over.shape[1:]), over.dtype)
+    operands = [spread, over, beside, across, master, momentum]
     return on_chip(kernel, operands, [whole, whole, piece, piece, piece, piece])
 
 
@@ -191,7 +178,7 @@
             side = kept_side() if kept else 1 - kept_side()
 
             def start(k, carry, j=j, src=src, first=first, proj=proj, side=side):
-                pltpu.make_async_copy(src.at[k], columns_of(out, proj, first + k, side), sems.at[j]).start()
+                pltpu.make_async_copy(src.at[k], columns_of(out, proj, 2 * (first + k) + side), sems.at[j]).start()
                 return carry
 
             lax.fori_loop(0, src.shape[0], start, 0, unroll=4)
@@ -219,29 +206,27 @@
 
 
 def step(local, master, momentum):
-    blocks = local.shape[2] // (2 * WIDTH)
-    sent = []
-    for first, count in ((0, CUT_IN), (CUT_IN, blocks - CUT_IN)):
-        theirs = swap(fetch(local, True, False, first, count), "c")
-        sent.append(swap(add(fetch(local, False, False, first, count), theirs), "xh"))
-    theirs = swap(fetch(local, True, True, 0, blocks), "c")
-    mine = fetch(local, False, True, 0, blocks)
-    summed = add_kept(mine, theirs, sent)
-
-    spread = exchange(summed)
+    theirs = swap(fetch(local, True), "c")
+    summed = add(fetch(local, False), theirs)
+
+    spread = exchange(summed, FSDP)
     spread = spread.reshape(2, 2, -1, *spread.shape[1:])
-    moved = across_rows(*part_rows(spread))
-    updated, velocity, own, over, beside, across = update(spread, *moved, master, momentum)
+    over, beside_other, beside_own = part_rows(spread)
+    over = swap(over, "xh")
+    across = swap(swap(beside_other, "c"), "xh")
+    beside = swap(beside_own, "c")
+    updated, velocity, own, over, beside, across = update(spread, over, beside, across, master, momentum)
 
     moved = across_rows(over, across, beside)
-    kept = exchange(join_rows(own, *moved).reshape(summed.shape))
-    early, late = swap(kept[:CUT_OUT], "xh"), swap(kept[CUT_OUT:], "xh")
+    joined = join_rows(own, *moved)
+    kept = exchange(joined.reshape(-1, *joined.shape[3:]), PLANE)
+    early, late = swap(kept[:CUT], "xh"), swap(kept[CUT:], "xh")
     pieces = [(kept, 0, False, True), (swap(kept, "c"), 0, True, True)]
     params = place(pieces)
     updated, velocity = store(updated, velocity)
     early, params, updated, velocity = lax.optimization_barrier((early, params, updated, velocity))
     params = place([(early, 0, False, False), (swap(early, "c"), 0, True, False)], params)
-    params = place([(late, CUT_OUT, False, False), (swap(late, "c"), CUT_OUT, True, False)], params)
+    params = place([(late, CUT, False, False), (swap(late, "c"), CUT, True, False)], params)
     return updated, velocity, params
 
 

time: 116 us -> 120 us (1.034)
  blocking collectives: 45.6 us -> 59.4 us
  starting transfers between devices: 21.9 us -> 18.3 us
  Pallas kernels: 10.4 us -> 7.21 us
  waiting for transfers between devices: 36.2 us -> 33.8 us
    all_to_all x2, blocking collectives: 45.6 us -> 59.4 us  [exchange(): return lax.all_to_all(value, axes, split_axis=0, concat_axis=0, tiled=True)]
    ppermute x16 -> x13, starting transfers between devices: 21.9 us -> 18.3 us  [swap(): return lax.ppermute(value, AXES, pairs(flip))]
    pallas_call x16 -> x10, Pallas kernels: 10.4 us -> 7.21 us  [on_chip(): pl.pallas_call(kernel, in_specs=[FAR if k in far else NEAR for k in range...]
    ppermute x16 -> x13, waiting for transfers between devices: 36.2 us -> 33.8 us  [swap(): return lax.ppermute(value, AXES, pairs(flip))]
  transfers between devices with their start and end apart: 16 -> 13, of which waited for: 7 -> 8; matrix products, arithmetic and copies ran while one was open for 0% -> 0% of each run, Pallas kernels for 7% -> 4%
where the time goes in v1:
time: 120 us; the launch traced here: 119 us
  blocking collectives  59.4 us (50%)
  waiting for transfers between devices  33.8 us (28%)
  starting transfers between devices  18.3 us (15%)
  Pallas kernels  7.21 us (6%)
    all_to_all x2, blocking collectives, exchange(): return lax.all_to_all(value, axes, split_axis=0, concat_axis=0, tiled=True)  59.4 us
    ppermute x13, waiting for transfers between devices, swap(): return lax.ppermute(value, AXES, pairs(flip))  33.8 us
    ppermute x13, starting transfers between devices, swap(): return lax.ppermute(value, AXES, pairs(flip))  18.3 us
    pallas_call x10, Pallas kernels, on_chip(): pl.pallas_call(kernel, in_specs=[FAR if k in far else NEAR for k in range...  7.21 us
  transfers between devices with their start and end apart: 13, of which 8 were waited for; matrix products, arithmetic and copies ran while one was open for 0% of the time, Pallas kernels for 4%

profile of v1, /device:TPU:1, one launch (start us, length us, event | category | flops | bytes accessed | tf_op | source)
XLA Modules:
  0.0 119.4 jit_solution(17929551727526977380)
XLA Ops:
  0.6 1.2 %shard_map.59 = bf16[64,32,256]{2,1,0:T(8,128)(2,1)S(1)} custom-call(bf16[2,32,16384]{2,1,0:T(8,128)(2,1)} %bitcast.6), custom_call_target="tpu_custom_call" | custom-call | tf_op jit(solution)/shard_map/pallas_call | solution.py:55
  1.9 3.3 %collective-permute-start = (bf16[64,32,256]{2,1,0:T(8,128)(2,1)S(1)}, bf16[64,32,256]{2,1,0:T(8,128)(2,1)S(1)}, u32[]{:S(2)}, u32[]{:S(2)}) collective-permute-start(bf16[64,32,256]{2,1,0:T(8,128)(2,1)S(1)} %shard_map.59), channel_id=1, source_target_pairs={{0,64},{1,65},{2,66},{3,67},{4,68},{5,69},{6,70},{7,71},{8,72},{9,... | collective-permute-start | bytes 3145736 | tf_op jit(solution)/shard_map/ppermute | solution.py:44
  5.2 1.2 %shard_map.58.refs_0_ = bf16[64,32,256]{2,1,0:T(8,128)(2,1)S(1)} custom-call(bf16[2,32,16384]{2,1,0:T(8,128)(2,1)} %bitcast.7), custom_call_target="tpu_custom_call" | custom-call | tf_op jit(solution)/shard_map/pallas_call | solution.py:55
  6.4 1.1 collective-permute-done.refs_1_
  7.5 0.3 shard_map.60
  7.8 0.0 copy-start
  7.8 0.0 copy-start.1
  7.8 37.6 %all_to_all.10 = bf16[64,32,256]{2,1,0:T(8,128)(2,1)S(1)} all-to-all(bf16[64,32,256]{2,1,0:T(8,128)(2,1)S(1)} %shard_map.60), channel_id=1, replica_groups=mesh['xh'=2,'c'=2,'zh'=2,'zm'=2,'z0'=2,'y'=4,'xl'=2] {'zh','zm','z0','y'..., dimensions={0} | all-to-all | bytes 2097152 | tf_op jit(solution)/shard_map/all_to_all | solution.py:48
  45.4 0.1 shard_map.61
  45.5 3.0 %collective-permute-start.3 = (bf16[16,32,256]{2,1,0:T(8,128)(2,1)S(1)}, bf16[16,32,256]{2,1,0:T(8,128)(2,1)S(1)}, u32[]{:S(2)}, u32[]{:S(2)}) collective-permute-start(bf16[16,32,256]{2,1,0:T(8,128)(2,1)S(1)} %get-tuple-element.20), channel_id=1, source_target_pairs={{0,64},{1,65},{2,66},{3,67},{4,68},{5,69},{6,70},{7,71},{8,72},{9,... | collective-permute-start | bytes 786440 | tf_op jit(solution)/shard_map/ppermute | solution.py:44
  48.4 2.5 %collective-permute-start.1 = (bf16[16,32,256]{2,1,0:T(8,128)(2,1)S(1)}, bf16[16,32,256]{2,1,0:T(8,128)(2,1)S(1)}, u32[]{:S(2)}, u32[]{:S(2)}) collective-permute-start(bf16[16,32,256]{2,1,0:T(8,128)(2,1)S(1)} %get-tuple-element.18), channel_id=1, source_target_pairs={{0,128},{1,129},{2,130},{3,131},{4,132},{5,133},{6,134},{7,135},{8... | collective-permute-start | bytes 786440 | tf_op jit(solution)/shard_map/ppermute | solution.py:44
  50.9 0.4 collective-permute-start.2
  51.2 0.0 collective-permute-done.3
  51.2 0.8 collective-permute-start.4
  52.0 5.7 %collective-permute-done.1.over_ref = bf16[16,32,256]{2,1,0:T(8,128)(2,1)S(1)} collective-permute-done((bf16[16,32,256]{2,1,0:T(8,128)(2,1)S(1)}, bf16[16,32,256]{2,1,0:T(8,128)(2,1)S(1)}, u32[]{:S(2)}, u32[]{:S(2)}) %collective-permute-start.1) | collective-permute-done | bytes 262176 | tf_op jit(solution)/shard_map/ppermute | solution.py:44
  57.7 0.0 collective-permute-done.2.beside_ref
  57.7 5.6 %collective-permute-done.4.across_ref = bf16[16,32,256]{2,1,0:T(8,128)(2,1)S(1)} collective-permute-done((bf16[16,32,256]{2,1,0:T(8,128)(2,1)S(1)}, bf16[16,32,256]{2,1,0:T(8,128)(2,1)S(1)}, u32[]{:S(2)}, u32[]{:S(2)}) %collective-permute-start.4) | collective-permute-done | bytes 262176 | tf_op jit(solution)/shard_map/ppermute | solution.py:44
  63.3 0.0 copy-done
  63.3 0.0 copy-done.1
  63.3 0.5 shard_map.62
  63.8 2.0 %collective-permute-start.5 = (bf16[8,32,256]{2,1,0:T(8,128)(2,1)S(1)}, bf16[8,32,256]{2,1,0:T(8,128)(2,1)S(1)}, u32[]{:S(2)}, u32[]{:S(2)}) collective-permute-start(bf16[8,32,256]{2,1,0:T(8,128)(2,1)S(1)} %get-tuple-element.22), channel_id=1, source_target_pairs={{0,129},{1,128},{2,131},{3,130},{4,133},{5,132},{6,135},{7,134},{8... | collective-permute-start | bytes 393224 | tf_op jit(solution)/shard_map/ppermute | solution.py:44
  65.8 1.9 %collective-permute-start.6 = (bf16[8,32,256]{2,1,0:T(8,128)(2,1)S(1)}, bf16[8,32,256]{2,1,0:T(8,128)(2,1)S(1)}, u32[]{:S(2)}, u32[]{:S(2)}) collective-permute-start(bf16[8,32,256]{2,1,0:T(8,128)(2,1)S(1)} %get-tuple-element.23), channel_id=1, source_target_pairs={{0,193},{1,192},{2,195},{3,194},{4,197},{5,196},{6,199},{7,198},{8... | collective-permute-start | bytes 393224 | tf_op jit(solution)/shard_map/ppermute | solution.py:44
  67.7 0.0 collective-permute-start.7
  67.7 1.2 %collective-permute-done.5.over_ref = bf16[8,32,256]{2,1,0:T(8,128)(2,1)S(1)} collective-permute-done((bf16[8,32,256]{2,1,0:T(8,128)(2,1)S(1)}, bf16[8,32,256]{2,1,0:T(8,128)(2,1)S(1)}, u32[]{:S(2)}, u32[]{:S(2)}) %collective-permute-start.5) | collective-permute-done | bytes 131104 | tf_op jit(solution)/shard_map/ppermute | solution.py:44
  68.9 4.3 %collective-permute-done.6.across_ref = bf16[8,32,256]{2,1,0:T(8,128)(2,1)S(1)} collective-permute-done((bf16[8,32,256]{2,1,0:T(8,128)(2,1)S(1)}, bf16[8,32,256]{2,1,0:T(8,128)(2,1)S(1)}, u32[]{:S(2)}, u32[]{:S(2)}) %collective-permute-start.6) | collective-permute-done | bytes 131104 | tf_op jit(solution)/shard_map/ppermute | solution.py:44
  73.2 0.0 collective-permute-done.7.beside_ref
  73.3 21.8 %all_to_all.11.refs_0_ = bf16[32,32,256]{2,1,0:T(8,128)(2,1)S(1)} all-to-all(bf16[32,32,256]{2,1,0:T(8,128)(2,1)S(1)} %bitcast.5), channel_id=1, replica_groups=mesh['xh'=2,'c'=2,'zh'=2,'zm'=2,'z0'=2,'y'=4,'xl'=2] {'zh','zm','z0','y'}, dimensions={0} | all-to-all | bytes 1048576 | tf_op jit(solution)/shard_map/all_to_all | solution.py:48
  95.0 2.1 %collective-permute-start.9 = (bf16[32,32,256]{2,1,0:T(8,128)(2,1)S(1)}, bf16[32,32,256]{2,1,0:T(8,128)(2,1)S(1)}, u32[]{:S(2)}, u32[]{:S(2)}) collective-permute-start(bf16[32,32,256]{2,1,0:T(8,128)(2,1)S(1)} %all_to_all.11.refs_0_), channel_id=1, source_target_pairs={{0,64},{1,65},{2,66},{3,67},{4,68},{5,69},{6,70},{7,71},{8,72},{9,... | collective-permute-start | bytes 1572872 | tf_op jit(solution)/shard_map/ppermute | solution.py:44
  97.1 0.4 collective-permute-start.8
  97.5 1.3 %shard_map.65 = (f32[2,512,256]{2,1,0:T(8,128)}, f32[2,512,256]{2,1,0:T(8,128)}) custom-call(f32[2,512,256]{2,1,0:T(8,128)S(1)} %get-tuple-element.25.first_ref, f32[2,512,256]{2,1,0:T(8,128)S(1)} %get-tuple-element.26.second_ref), custom_call_target="tpu_custom_call" | custom-call | tf_op jit(solution)/shard_map/pallas_call | solution.py:55
  98.8 0.0 collective-permute-done.9.refs_1_
  98.8 1.0 shard_map.64.refs_2_
  99.8 9.6 %collective-permute-done.8.refs_0_ = bf16[24,32,256]{2,1,0:T(8,128)(2,1)S(1)} collective-permute-done((bf16[24,32,256]{2,1,0:T(8,128)(2,1)S(1)}, bf16[24,32,256]{2,1,0:T(8,128)(2,1)S(1)}, u32[]{:S(2)}, u32[]{:S(2)}) %collective-permute-start.8) | collective-permute-done | bytes 393248 | tf_op jit(solution)/shard_map/ppermute | solution.py:44
  109.4 0.9 collective-permute-start.12
  110.3 0.4 collective-permute-start.10
  110.6 6.3 %collective-permute-done.10.refs_0_ = bf16[8,32,256]{2,1,0:T(8,128)(2,1)S(1)} collective-permute-done((bf16[8,32,256]{2,1,0:T(8,128)(2,1)S(1)}, bf16[8,32,256]{2,1,0:T(8,128)(2,1)S(1)}, u32[]{:S(2)}, u32[]{:S(2)}) %collective-permute-start.10) | collective-permute-done | bytes 131104 | tf_op jit(solution)/shard_map/ppermute | solution.py:44
  116.9 0.9 collective-permute-start.11
  117.8 0.0 collective-permute-done.12.refs_1_
  117.8 0.9 shard_map.66.refs_2_
  118.6 0.1 collective-permute-done.11.refs_1_
  118.7 0.7 shard_map.67
  (3 shorter events, 0.1 us)
Async XLA Ops:
  1.9 5.6 %collective-permute-start = (bf16[64,32,256]{2,1,0:T(8,128)(2,1)S(1)}, bf16[64,32,256]{2,1,0:T(8,128)(2,1)S(1)}, u32[]{:S(2)}, u32[]{:S(2)}) collective-permute-start(bf16[64,32,256]{2,1,0:T(8,128)(2,1)S(1)} %shard_map.59), channel_id=1, source_target_pairs={{0,64},{1,65},{2,66},{3,67},{4,68},{5,69},{6,70},{7,71},{8,72},{9,... | collective-permute-start | bytes 3145736 | tf_op jit(solution)/shard_map/ppermute | solution.py:44
  7.8 55.5 %copy-start = (f32[2,512,256]{2,1,0:T(8,128)S(1)}, f32[2,512,256]{2,1,0:T(8,128)}, u32[]{:S(2)}) copy-start(f32[2,512,256]{2,1,0:T(8,128)} %m_ref.1) | copy-start | bytes 3145732
  7.8 55.5 %copy-start.1 = (f32[2,512,256]{2,1,0:T(8,128)S(1)}, f32[2,512,256]{2,1,0:T(8,128)}, u32[]{:S(2)}) copy-start(f32[2,512,256]{2,1,0:T(8,128)} %v_ref.1) | copy-start | bytes 3145732
  45.5 5.8 %collective-permute-start.3 = (bf16[16,32,256]{2,1,0:T(8,128)(2,1)S(1)}, bf16[16,32,256]{2,1,0:T(8,128)(2,1)S(1)}, u32[]{:S(2)}, u32[]{:S(2)}) collective-permute-start(bf16[16,32,256]{2,1,0:T(8,128)(2,1)S(1)} %get-tuple-element.20), channel_id=1, source_target_pairs={{0,64},{1,65},{2,66},{3,67},{4,68},{5,69},{6,70},{7,71},{8,72},{9,... | collective-permute-start | bytes 786440 | tf_op jit(solution)/shard_map/ppermute | solution.py:44
  48.4 9.3 %collective-permute-start.1 = (bf16[16,32,256]{2,1,0:T(8,128)(2,1)S(1)}, bf16[16,32,256]{2,1,0:T(8,128)(2,1)S(1)}, u32[]{:S(2)}, u32[]{:S(2)}) collective-permute-start(bf16[16,32,256]{2,1,0:T(8,128)(2,1)S(1)} %get-tuple-element.18), channel_id=1, source_target_pairs={{0,128},{1,129},{2,130},{3,131},{4,132},{5,133},{6,134},{7,135},{8... | collective-permute-start | bytes 786440 | tf_op jit(solution)/shard_map/ppermute | solution.py:44
  50.9 6.8 %collective-permute-start.2 = (bf16[16,32,256]{2,1,0:T(8,128)(2,1)S(1)}, bf16[16,32,256]{2,1,0:T(8,128)(2,1)S(1)}, u32[]{:S(2)}, u32[]{:S(2)}) collective-permute-start(bf16[16,32,256]{2,1,0:T(8,128)(2,1)S(1)} %get-tuple-element.19), channel_id=1, source_target_pairs={{0,64},{1,65},{2,66},{3,67},{4,68},{5,69},{6,70},{7,71},{8,72},{9,... | collective-permute-start | bytes 786440 | tf_op jit(solution)/shard_map/ppermute | solution.py:44
  51.2 12.0 %collective-permute-start.4 = (bf16[16,32,256]{2,1,0:T(8,128)(2,1)S(1)}, bf16[16,32,256]{2,1,0:T(8,128)(2,1)S(1)}, u32[]{:S(2)}, u32[]{:S(2)}) collective-permute-start(bf16[16,32,256]{2,1,0:T(8,128)(2,1)S(1)} %collective-permute-done.3), channel_id=1, source_target_pairs={{0,128},{1,129},{2,130},{3,131},{4,132},{5,133},{6,134},{7,135},{8... | collective-permute-start | bytes 786440 | tf_op jit(solution)/shard_map/ppermute | solution.py:44
  63.8 5.1 %collective-permute-start.5 = (bf16[8,32,256]{2,1,0:T(8,128)(2,1)S(1)}, bf16[8,32,256]{2,1,0:T(8,128)(2,1)S(1)}, u32[]{:S(2)}, u32[]{:S(2)}) collective-permute-start(bf16[8,32,256]{2,1,0:T(8,128)(2,1)S(1)} %get-tuple-element.22), channel_id=1, source_target_pairs={{0,129},{1,128},{2,131},{3,130},{4,133},{5,132},{6,135},{7,134},{8... | collective-permute-start | bytes 393224 | tf_op jit(solution)/shard_map/ppermute | solution.py:44
  65.8 7.4 %collective-permute-start.6 = (bf16[8,32,256]{2,1,0:T(8,128)(2,1)S(1)}, bf16[8,32,256]{2,1,0:T(8,128)(2,1)S(1)}, u32[]{:S(2)}, u32[]{:S(2)}) collective-permute-start(bf16[8,32,256]{2,1,0:T(8,128)(2,1)S(1)} %get-tuple-element.23), channel_id=1, source_target_pairs={{0,193},{1,192},{2,195},{3,194},{4,197},{5,196},{6,199},{7,198},{8... | collective-permute-start | bytes 393224 | tf_op jit(solution)/shard_map/ppermute | solution.py:44
  67.7 5.5 %collective-permute-start.7 = (bf16[8,32,256]{2,1,0:T(8,128)(2,1)S(1)}, bf16[8,32,256]{2,1,0:T(8,128)(2,1)S(1)}, u32[]{:S(2)}, u32[]{:S(2)}) collective-permute-start(bf16[8,32,256]{2,1,0:T(8,128)(2,1)S(1)} %get-tuple-element.24), channel_id=1, source_target_pairs={{0,64},{1,65},{2,66},{3,67},{4,68},{5,69},{6,70},{7,71},{8,72},{9,... | collective-permute-start | bytes 393224 | tf_op jit(solution)/shard_map/ppermute | solution.py:44
  95.0 3.8 %collective-permute-start.9 = (bf16[32,32,256]{2,1,0:T(8,128)(2,1)S(1)}, bf16[32,32,256]{2,1,0:T(8,128)(2,1)S(1)}, u32[]{:S(2)}, u32[]{:S(2)}) collective-permute-start(bf16[32,32,256]{2,1,0:T(8,128)(2,1)S(1)} %all_to_all.11.refs_0_), channel_id=1, source_target_pairs={{0,64},{1,65},{2,66},{3,67},{4,68},{5,69},{6,70},{7,71},{8,72},{9,... | collective-permute-start | bytes 1572872 | tf_op jit(solution)/shard_map/ppermute | solution.py:44
  97.1 12.3 %collective-permute-start.8 = (bf16[24,32,256]{2,1,0:T(8,128)(2,1)S(1)}, bf16[24,32,256]{2,1,0:T(8,128)(2,1)S(1)}, u32[]{:S(2)}, u32[]{:S(2)}) collective-permute-start(bf16[24,32,256]{2,1,0:T(8,128)(2,1)S(1)} %slice.8), channel_id=1, source_target_pairs={{0,128},{1,129},{2,130},{3,131},{4,132},{5,133},{6,134},{7,135},{8... | collective-permute-start | bytes 1179656 | tf_op jit(solution)/shard_map/ppermute | solution.py:44
  109.4 8.4 %collective-permute-start.12 = (bf16[24,32,256]{2,1,0:T(8,128)(2,1)S(1)}, bf16[24,32,256]{2,1,0:T(8,128)(2,1)S(1)}, u32[]{:S(2)}, u32[]{:S(2)}) collective-permute-start(bf16[24,32,256]{2,1,0:T(8,128)(2,1)S(1)} %collective-permute-done.8.refs_0_), channel_id=1, source_target_pairs={{0,64},{1,65},{2,66},{3,67},{4,68},{5,69},{6,70},{7,71},{8,72},{9,... | collective-permute-start | bytes 1179656 | tf_op jit(solution)/shard_map/ppermute | solution.py:44
  110.3 6.6 %collective-permute-start.10 = (bf16[8,32,256]{2,1,0:T(8,128)(2,1)S(1)}, bf16[8,32,256]{2,1,0:T(8,128)(2,1)S(1)}, u32[]{:S(2)}, u32[]{:S(2)}) collective-permute-start(bf16[8,32,256]{2,1,0:T(8,128)(2,1)S(1)} %slice.9), channel_id=1, source_target_pairs={{0,128},{1,129},{2,130},{3,131},{4,132},{5,133},{6,134},{7,135},{8... | collective-permute-start | bytes 393224 | tf_op jit(solution)/shard_map/ppermute | solution.py:44
  116.9 1.8 %collective-permute-start.11 = (bf16[8,32,256]{2,1,0:T(8,128)(2,1)S(1)}, bf16[8,32,256]{2,1,0:T(8,128)(2,1)S(1)}, u32[]{:S(2)}, u32[]{:S(2)}) collective-permute-start(bf16[8,32,256]{2,1,0:T(8,128)(2,1)S(1)} %collective-permute-done.10.refs_0_), channel_id=1, source_target_pairs={{0,64},{1,65},{2,66},{3,67},{4,68},{5,69},{6,70},{7,71},{8,72},{9,... | collective-permute-start | bytes 393224 | tf_op jit(solution)/shard_map/ppermute | solution.py:44

commit v2 on v0

--- a/solution.py
+++ b/solution.py
@@ -15,7 +15,7 @@
 FSDP = ("zh", "zm", "z0", "y", "xl")
 WIDTH = 256
 COLUMNS = 64 * WIDTH
-CUT_IN, CUT_OUT = 12, 24
+CUT = 24
 GRANT = 8 << 20
 
 
@@ -69,19 +69,22 @@
     return ref.at[proj, :, pl.ds(pl.multiple_of((2 * k + side) * WIDTH, WIDTH), WIDTH)]
 
 
-def fetch(deltas, other_core, kept, first, count):
+def fetch(deltas, other_core, kept):
+    _, rows, columns = deltas.shape
+    blocks = columns // (2 * WIDTH)
+
     def kernel(src, out, sem):
         proj = 1 - index("c") if other_core else index("c")
         side = kept_side() if kept else 1 - kept_side()
 
         def start(k, carry):
-            pltpu.make_async_copy(columns_of(src, proj, first + k, side), out.at[k], sem).start()
+            pltpu.make_async_copy(columns_of(src, proj, k, side), out.at[k], sem).start()
             return carry
 
-        lax.fori_loop(0, count, start, 0, unroll=4)
+        lax.fori_loop(0, blocks, start, 0, unroll=4)
         pltpu.make_async_copy(out, out, sem).wait()
 
-    out = ((count, deltas.shape[1], WIDTH), deltas.dtype)
+    out = ((blocks, rows, WIDTH), deltas.dtype)
     return on_chip(kernel, [deltas], [out], far=(0,), scratch=[pltpu.SemaphoreType.DMA])[0]
 
 
@@ -99,23 +102,6 @@
         lax.fori_loop(0, out.shape[0], body, 0, unroll=4)
 
     return on_chip(kernel, values, [(values[0].shape, values[0].dtype)])[0]
-
-
-def add_kept(mine, theirs, sent):
-    def kernel(mine_ref, theirs_ref, *refs):
-        *parts, out = refs
-        first = 0
-        for part in parts:
-
-            def body(k, carry, part=part, first=first):
-                total = mine_ref[first + k].astype(jnp.float32) + theirs_ref[first + k].astype(jnp.float32)
-                out[first + k] = (total + part[k].astype(jnp.float32)).astype(out.dtype)
-                return carry
-
-            lax.fori_loop(0, part.shape[0], body, 0, unroll=4)
-            first += part.shape[0]
-
-    return on_chip(kernel, [mine, theirs, *sent], [(mine.shape, mine.dtype)])[0]
 
 
 def part_rows(spread):
@@ -219,14 +205,11 @@
 
 
 def step(local, master, momentum):
-    blocks = local.shape[2] // (2 * WIDTH)
-    sent = []
-    for first, count in ((0, CUT_IN), (CUT_IN, blocks - CUT_IN)):
-        theirs = swap(fetch(local, True, False, first, count), "c")
-        sent.append(swap(add(fetch(local, False, False, first, count), theirs), "xh"))
-    theirs = swap(fetch(local, True, True, 0, blocks), "c")
-    mine = fetch(local, False, True, 0, blocks)
-    summed = add_kept(mine, theirs, sent)
+    theirs = swap(fetch(local, True, False), "c")
+    sent = swap(add(fetch(local, False, False), theirs), "xh")
+    theirs = swap(fetch(local, True, True), "c")
+    mine = fetch(local, False, True)
+    summed = add(mine, theirs, sent)
 
     spread = exchange(summed)
     spread = spread.reshape(2, 2, -1, *spread.shape[1:])
@@ -234,14 +217,14 @@
     updated, velocity, own, over, beside, across = update(spread, *moved, master, momentum)
 
     moved = across_rows(over, across, beside)
+    updated, velocity = store(updated, velocity)
     kept = exchange(join_rows(own, *moved).reshape(summed.shape))
-    early, late = swap(kept[:CUT_OUT], "xh"), swap(kept[CUT_OUT:], "xh")
+    early, late = swap(kept[:CUT], "xh"), swap(kept[CUT:], "xh")
     pieces = [(kept, 0, False, True), (swap(kept, "c"), 0, True, True)]
     params = place(pieces)
-    updated, velocity = store(updated, velocity)
-    early, params, updated, velocity = lax.optimization_barrier((early, params, updated, velocity))
+    early, params = lax.optimization_barrier((early, params))
     params = place([(early, 0, False, False), (swap(early, "c"), 0, True, False)], params)
-    params = place([(late, CUT_OUT, False, False), (swap(late, "c"), CUT_OUT, True, False)], params)
+    params = place([(late, CUT, False, False), (swap(late, "c"), CUT, True, False)], params)
     return updated, velocity, params
 
 

time: 116 us -> 115 us (level)
  waiting for transfers between devices: 36.2 us -> 40.1 us
  starting transfers between devices: 21.9 us -> 19.4 us
  Pallas kernels: 10.4 us -> 8.83 us
    ppermute x16 -> x14, waiting for transfers between devices: 36.2 us -> 40.1 us  [swap(): return lax.ppermute(value, AXES, pairs(flip))]
    ppermute x16 -> x14, starting transfers between devices: 21.9 us -> 19.4 us  [swap(): return lax.ppermute(value, AXES, pairs(flip))]
    pallas_call x16 -> x13, Pallas kernels: 10.4 us -> 8.83 us  [on_chip(): pl.pallas_call(kernel, in_specs=[FAR if k in far else NEAR for k in range...]
  transfers between devices with their start and end apart: 16 -> 14, of which waited for: 7 -> 7; matrix products, arithmetic and copies ran while one was open for 0% -> 0% of each run, Pallas kernels for 7% -> 6%
where the time goes in v2:
time: 115 us
  blocking collectives  45.6 us (40%)
  waiting for transfers between devices  40.1 us (35%)
  starting transfers between devices  19.4 us (17%)
  Pallas kernels  8.83 us (8%)
    all_to_all x2, blocking collectives, exchange(): return lax.all_to_all(value, PLANE, split_axis=0, concat_axis=0, tiled=True)  45.6 us
    ppermute x14, waiting for transfers between devices, swap(): return lax.ppermute(value, AXES, pairs(flip))  40.1 us
    ppermute x14, starting transfers between devices, swap(): return lax.ppermute(value, AXES, pairs(flip))  19.4 us
    pallas_call x13, Pallas kernels, on_chip(): pl.pallas_call(kernel, in_specs=[FAR if k in far else NEAR for k in range...  8.83 us
  transfers between devices with their start and end apart: 14, of which 7 were waited for; matrix products, arithmetic and copies ran while one was open for 0% of the time, Pallas kernels for 6%

profile of v2, /device:TPU:1, one launch (start us, length us, event | category | flops | bytes accessed | tf_op | source)
XLA Modules:
  0.0 114.8 jit_solution(8940102484802959647)
XLA Ops:
  0.6 1.0 shard_map.61
  1.7 3.3 %collective-permute-start.1 = (bf16[32,32,256]{2,1,0:T(8,128)(2,1)S(1)}, bf16[32,32,256]{2,1,0:T(8,128)(2,1)S(1)}, u32[]{:S(2)}, u32[]{:S(2)}) collective-permute-start(bf16[32,32,256]{2,1,0:T(8,128)(2,1)S(1)} %shard_map.61), channel_id=1, source_target_pairs={{0,64},{1,65},{2,66},{3,67},{4,68},{5,69},{6,70},{7,71},{8,72},{9,... | collective-permute-start | bytes 1572872 | tf_op jit(solution)/shard_map/ppermute | solution.py:44
  5.0 1.0 shard_map.59
  6.0 0.1 collective-permute-start
  6.1 1.0 shard_map.60.refs_0_
  7.1 0.0 collective-permute-done.1.refs_1_
  7.1 0.2 shard_map.62
  7.3 1.1 collective-permute-start.2
  8.4 1.0 shard_map.58.refs_0_
  9.4 0.0 copy-start
  9.5 0.0 copy-start.1
  9.5 0.0 collective-permute-done.refs_1_
  9.5 12.4 %collective-permute-done.2.refs_2_ = bf16[32,32,256]{2,1,0:T(8,128)(2,1)S(1)} collective-permute-done((bf16[32,32,256]{2,1,0:T(8,128)(2,1)S(1)}, bf16[32,32,256]{2,1,0:T(8,128)(2,1)S(1)}, u32[]{:S(2)}, u32[]{:S(2)}) %collective-permute-start.2) | collective-permute-done | bytes 524320 | tf_op jit(solution)/shard_map/ppermute | solution.py:44
  21.9 0.2 shard_map.63
  22.2 24.7 %all_to_all.10 = bf16[32,32,256]{2,1,0:T(8,128)(2,1)S(1)} all-to-all(bf16[32,32,256]{2,1,0:T(8,128)(2,1)S(1)} %shard_map.63), channel_id=1, replica_groups=mesh['xh'=2,'c'=2,'zh'=2,'zm'=2,'z0'=2,'y'=4,'xl'=2] {'zh','zm','z0','y'}, dimensions={0} | all-to-all | bytes 1048576 | tf_op jit(solution)/shard_map/all_to_all | solution.py:48
  46.9 2.6 %collective-permute-start.3 = (bf16[8,32,256]{2,1,0:T(8,128)(2,1)S(1)}, bf16[8,32,256]{2,1,0:T(8,128)(2,1)S(1)}, u32[]{:S(2)}, u32[]{:S(2)}) collective-permute-start(bf16[8,32,256]{2,1,0:T(8,128)(2,1)S(1)} %get-tuple-element.16), channel_id=1, source_target_pairs={{0,129},{1,128},{2,131},{3,130},{4,133},{5,132},{6,135},{7,134},{8... | collective-permute-start | bytes 393224 | tf_op jit(solution)/shard_map/ppermute | solution.py:44
  49.5 3.7 %collective-permute-start.4 = (bf16[8,32,256]{2,1,0:T(8,128)(2,1)S(1)}, bf16[8,32,256]{2,1,0:T(8,128)(2,1)S(1)}, u32[]{:S(2)}, u32[]{:S(2)}) collective-permute-start(bf16[8,32,256]{2,1,0:T(8,128)(2,1)S(1)} %get-tuple-element.17), channel_id=1, source_target_pairs={{0,193},{1,192},{2,195},{3,194},{4,197},{5,196},{6,199},{7,198},{8... | collective-permute-start | bytes 393224 | tf_op jit(solution)/shard_map/ppermute | solution.py:44
  53.2 0.0 collective-permute-start.5
  53.2 0.0 collective-permute-done.3.over_ref
  53.2 5.0 %collective-permute-done.4.across_ref = bf16[8,32,256]{2,1,0:T(8,128)(2,1)S(1)} collective-permute-done((bf16[8,32,256]{2,1,0:T(8,128)(2,1)S(1)}, bf16[8,32,256]{2,1,0:T(8,128)(2,1)S(1)}, u32[]{:S(2)}, u32[]{:S(2)}) %collective-permute-start.4) | collective-permute-done | bytes 131104 | tf_op jit(solution)/shard_map/ppermute | solution.py:44
  58.2 0.0 collective-permute-done.5.beside_ref
  58.2 0.0 copy-done
  58.2 0.0 copy-done.1
  58.2 0.4 shard_map.65
  58.6 3.0 %collective-permute-start.6 = (bf16[8,32,256]{2,1,0:T(8,128)(2,1)S(1)}, bf16[8,32,256]{2,1,0:T(8,128)(2,1)S(1)}, u32[]{:S(2)}, u32[]{:S(2)}) collective-permute-start(bf16[8,32,256]{2,1,0:T(8,128)(2,1)S(1)} %get-tuple-element.24), channel_id=1, source_target_pairs={{0,129},{1,128},{2,131},{3,130},{4,133},{5,132},{6,135},{7,134},{8... | collective-permute-start | bytes 393224 | tf_op jit(solution)/shard_map/ppermute | solution.py:44
  61.6 1.1 %collective-permute-start.7 = (bf16[8,32,256]{2,1,0:T(8,128)(2,1)S(1)}, bf16[8,32,256]{2,1,0:T(8,128)(2,1)S(1)}, u32[]{:S(2)}, u32[]{:S(2)}) collective-permute-start(bf16[8,32,256]{2,1,0:T(8,128)(2,1)S(1)} %get-tuple-element.25), channel_id=1, source_target_pairs={{0,193},{1,192},{2,195},{3,194},{4,197},{5,196},{6,199},{7,198},{8... | collective-permute-start | bytes 393224 | tf_op jit(solution)/shard_map/ppermute | solution.py:44
  62.7 0.0 collective-permute-start.8
  62.7 2.2 %collective-permute-done.6.over_ref = bf16[8,32,256]{2,1,0:T(8,128)(2,1)S(1)} collective-permute-done((bf16[8,32,256]{2,1,0:T(8,128)(2,1)S(1)}, bf16[8,32,256]{2,1,0:T(8,128)(2,1)S(1)}, u32[]{:S(2)}, u32[]{:S(2)}) %collective-permute-start.6) | collective-permute-done | bytes 131104 | tf_op jit(solution)/shard_map/ppermute | solution.py:44
  64.9 3.3 %collective-permute-done.7.across_ref = bf16[8,32,256]{2,1,0:T(8,128)(2,1)S(1)} collective-permute-done((bf16[8,32,256]{2,1,0:T(8,128)(2,1)S(1)}, bf16[8,32,256]{2,1,0:T(8,128)(2,1)S(1)}, u32[]{:S(2)}, u32[]{:S(2)}) %collective-permute-start.7) | collective-permute-done | bytes 131104 | tf_op jit(solution)/shard_map/ppermute | solution.py:44
  68.2 0.0 collective-permute-done.8.beside_ref
  68.2 20.8 %all_to_all.11.refs_0_ = bf16[32,32,256]{2,1,0:T(8,128)(2,1)S(1)} all-to-all(bf16[32,32,256]{2,1,0:T(8,128)(2,1)S(1)} %bitcast.5), channel_id=1, replica_groups=mesh['xh'=2,'c'=2,'zh'=2,'zm'=2,'z0'=2,'y'=4,'xl'=2] {'zh','zm','z0','y'}, dimensions={0} | all-to-all | bytes 1048576 | tf_op jit(solution)/shard_map/all_to_all | solution.py:48
  89.1 2.1 %collective-permute-start.12 = (bf16[32,32,256]{2,1,0:T(8,128)(2,1)S(1)}, bf16[32,32,256]{2,1,0:T(8,128)(2,1)S(1)}, u32[]{:S(2)}, u32[]{:S(2)}) collective-permute-start(bf16[32,32,256]{2,1,0:T(8,128)(2,1)S(1)} %all_to_all.11.refs_0_), channel_id=1, source_target_pairs={{0,64},{1,65},{2,66},{3,67},{4,68},{5,69},{6,70},{7,71},{8,72},{9,... | collective-permute-start | bytes 1572872 | tf_op jit(solution)/shard_map/ppermute | solution.py:44
  91.1 0.4 collective-permute-start.11
  91.5 1.1 collective-permute-done.12.refs_1_
  92.6 1.0 shard_map.68.refs_2_
  93.6 9.8 %collective-permute-done.11.refs_0_ = bf16[24,32,256]{2,1,0:T(8,128)(2,1)S(1)} collective-permute-done((bf16[24,32,256]{2,1,0:T(8,128)(2,1)S(1)}, bf16[24,32,256]{2,1,0:T(8,128)(2,1)S(1)}, u32[]{:S(2)}, u32[]{:S(2)}) %collective-permute-start.11) | collective-permute-done | bytes 393248 | tf_op jit(solution)/shard_map/ppermute | solution.py:44
  103.4 0.9 collective-permute-start.13
  104.3 0.4 collective-permute-start.9
  104.6 6.3 %collective-permute-done.9.refs_0_ = bf16[8,32,256]{2,1,0:T(8,128)(2,1)S(1)} collective-permute-done((bf16[8,32,256]{2,1,0:T(8,128)(2,1)S(1)}, bf16[8,32,256]{2,1,0:T(8,128)(2,1)S(1)}, u32[]{:S(2)}, u32[]{:S(2)}) %collective-permute-start.9) | collective-permute-done | bytes 131104 | tf_op jit(solution)/shard_map/ppermute | solution.py:44
  110.9 0.9 collective-permute-start.10
  111.8 1.3 %shard_map.66 = (f32[2,512,256]{2,1,0:T(8,128)}, f32[2,512,256]{2,1,0:T(8,128)}) custom-call(f32[2,512,256]{2,1,0:T(8,128)S(1)} %get-tuple-element.19.first_ref, f32[2,512,256]{2,1,0:T(8,128)S(1)} %get-tuple-element.20.second_ref), custom_call_target="tpu_custom_call" | custom-call | tf_op jit(solution)/shard_map/pallas_call | solution.py:55
  113.1 0.0 collective-permute-done.13.refs_1_
  113.1 0.9 shard_map.69.refs_2_
  114.0 0.0 collective-permute-done.10.refs_1_
  114.0 0.7 shard_map.70
  (4 shorter events, 0.1 us)
Async XLA Ops:
  1.7 5.5 %collective-permute-start.1 = (bf16[32,32,256]{2,1,0:T(8,128)(2,1)S(1)}, bf16[32,32,256]{2,1,0:T(8,128)(2,1)S(1)}, u32[]{:S(2)}, u32[]{:S(2)}) collective-permute-start(bf16[32,32,256]{2,1,0:T(8,128)(2,1)S(1)} %shard_map.61), channel_id=1, source_target_pairs={{0,64},{1,65},{2,66},{3,67},{4,68},{5,69},{6,70},{7,71},{8,72},{9,... | collective-permute-start | bytes 1572872 | tf_op jit(solution)/shard_map/ppermute | solution.py:44
  6.0 3.5 %collective-permute-start = (bf16[32,32,256]{2,1,0:T(8,128)(2,1)S(1)}, bf16[32,32,256]{2,1,0:T(8,128)(2,1)S(1)}, u32[]{:S(2)}, u32[]{:S(2)}) collective-permute-start(bf16[32,32,256]{2,1,0:T(8,128)(2,1)S(1)} %shard_map.59), channel_id=1, source_target_pairs={{0,64},{1,65},{2,66},{3,67},{4,68},{5,69},{6,70},{7,71},{8,72},{9,... | collective-permute-start | bytes 1572872 | tf_op jit(solution)/shard_map/ppermute | solution.py:44
  7.3 14.6 %collective-permute-start.2 = (bf16[32,32,256]{2,1,0:T(8,128)(2,1)S(1)}, bf16[32,32,256]{2,1,0:T(8,128)(2,1)S(1)}, u32[]{:S(2)}, u32[]{:S(2)}) collective-permute-start(bf16[32,32,256]{2,1,0:T(8,128)(2,1)S(1)} %shard_map.62), channel_id=1, source_target_pairs={{0,128},{1,129},{2,130},{3,131},{4,132},{5,133},{6,134},{7,135},{8... | collective-permute-start | bytes 1572872 | tf_op jit(solution)/shard_map/ppermute | solution.py:44
  9.4 48.7 %copy-start = (f32[2,512,256]{2,1,0:T(8,128)S(1)}, f32[2,512,256]{2,1,0:T(8,128)}, u32[]{:S(2)}) copy-start(f32[2,512,256]{2,1,0:T(8,128)} %m_ref.1) | copy-start | bytes 3145732
  9.5 48.7 %copy-start.1 = (f32[2,512,256]{2,1,0:T(8,128)S(1)}, f32[2,512,256]{2,1,0:T(8,128)}, u32[]{:S(2)}) copy-start(f32[2,512,256]{2,1,0:T(8,128)} %v_ref.1) | copy-start | bytes 3145732
  46.9 6.3 %collective-permute-start.3 = (bf16[8,32,256]{2,1,0:T(8,128)(2,1)S(1)}, bf16[8,32,256]{2,1,0:T(8,128)(2,1)S(1)}, u32[]{:S(2)}, u32[]{:S(2)}) collective-permute-start(bf16[8,32,256]{2,1,0:T(8,128)(2,1)S(1)} %get-tuple-element.16), channel_id=1, source_target_pairs={{0,129},{1,128},{2,131},{3,130},{4,133},{5,132},{6,135},{7,134},{8... | collective-permute-start | bytes 393224 | tf_op jit(solution)/shard_map/ppermute | solution.py:44
  49.5 8.7 %collective-permute-start.4 = (bf16[8,32,256]{2,1,0:T(8,128)(2,1)S(1)}, bf16[8,32,256]{2,1,0:T(8,128)(2,1)S(1)}, u32[]{:S(2)}, u32[]{:S(2)}) collective-permute-start(bf16[8,32,256]{2,1,0:T(8,128)(2,1)S(1)} %get-tuple-element.17), channel_id=1, source_target_pairs={{0,193},{1,192},{2,195},{3,194},{4,197},{5,196},{6,199},{7,198},{8... | collective-permute-start | bytes 393224 | tf_op jit(solution)/shard_map/ppermute | solution.py:44
  53.2 5.0 %collective-permute-start.5 = (bf16[8,32,256]{2,1,0:T(8,128)(2,1)S(1)}, bf16[8,32,256]{2,1,0:T(8,128)(2,1)S(1)}, u32[]{:S(2)}, u32[]{:S(2)}) collective-permute-start(bf16[8,32,256]{2,1,0:T(8,128)(2,1)S(1)} %get-tuple-element.18), channel_id=1, source_target_pairs={{0,64},{1,65},{2,66},{3,67},{4,68},{5,69},{6,70},{7,71},{8,72},{9,... | collective-permute-start | bytes 393224 | tf_op jit(solution)/shard_map/ppermute | solution.py:44
  58.6 6.3 %collective-permute-start.6 = (bf16[8,32,256]{2,1,0:T(8,128)(2,1)S(1)}, bf16[8,32,256]{2,1,0:T(8,128)(2,1)S(1)}, u32[]{:S(2)}, u32[]{:S(2)}) collective-permute-start(bf16[8,32,256]{2,1,0:T(8,128)(2,1)S(1)} %get-tuple-element.24), channel_id=1, source_target_pairs={{0,129},{1,128},{2,131},{3,130},{4,133},{5,132},{6,135},{7,134},{8... | collective-permute-start | bytes 393224 | tf_op jit(solution)/shard_map/ppermute | solution.py:44
  61.6 6.6 %collective-permute-start.7 = (bf16[8,32,256]{2,1,0:T(8,128)(2,1)S(1)}, bf16[8,32,256]{2,1,0:T(8,128)(2,1)S(1)}, u32[]{:S(2)}, u32[]{:S(2)}) collective-permute-start(bf16[8,32,256]{2,1,0:T(8,128)(2,1)S(1)} %get-tuple-element.25), channel_id=1, source_target_pairs={{0,193},{1,192},{2,195},{3,194},{4,197},{5,196},{6,199},{7,198},{8... | collective-permute-start | bytes 393224 | tf_op jit(solution)/shard_map/ppermute | solution.py:44
  62.7 5.5 %collective-permute-start.8 = (bf16[8,32,256]{2,1,0:T(8,128)(2,1)S(1)}, bf16[8,32,256]{2,1,0:T(8,128)(2,1)S(1)}, u32[]{:S(2)}, u32[]{:S(2)}) collective-permute-start(bf16[8,32,256]{2,1,0:T(8,128)(2,1)S(1)} %get-tuple-element.26), channel_id=1, source_target_pairs={{0,64},{1,65},{2,66},{3,67},{4,68},{5,69},{6,70},{7,71},{8,72},{9,... | collective-permute-start | bytes 393224 | tf_op jit(solution)/shard_map/ppermute | solution.py:44
  89.1 3.6 %collective-permute-start.12 = (bf16[32,32,256]{2,1,0:T(8,128)(2,1)S(1)}, bf16[32,32,256]{2,1,0:T(8,128)(2,1)S(1)}, u32[]{:S(2)}, u32[]{:S(2)}) collective-permute-start(bf16[32,32,256]{2,1,0:T(8,128)(2,1)S(1)} %all_to_all.11.refs_0_), channel_id=1, source_target_pairs={{0,64},{1,65},{2,66},{3,67},{4,68},{5,69},{6,70},{7,71},{8,72},{9,... | collective-permute-start | bytes 1572872 | tf_op jit(solution)/shard_map/ppermute | solution.py:44
  91.1 12.3 %collective-permute-start.11 = (bf16[24,32,256]{2,1,0:T(8,128)(2,1)S(1)}, bf16[24,32,256]{2,1,0:T(8,128)(2,1)S(1)}, u32[]{:S(2)}, u32[]{:S(2)}) collective-permute-start(bf16[24,32,256]{2,1,0:T(8,128)(2,1)S(1)} %slice.9), channel_id=1, source_target_pairs={{0,128},{1,129},{2,130},{3,131},{4,132},{5,133},{6,134},{7,135},{8... | collective-permute-start | bytes 1179656 | tf_op jit(solution)/shard_map/ppermute | solution.py:44
  103.4 9.7 %collective-permute-start.13 = (bf16[24,32,256]{2,1,0:T(8,128)(2,1)S(1)}, bf16[24,32,256]{2,1,0:T(8,128)(2,1)S(1)}, u32[]{:S(2)}, u32[]{:S(2)}) collective-permute-start(bf16[24,32,256]{2,1,0:T(8,128)(2,1)S(1)} %collective-permute-done.11.refs_0_), channel_id=1, source_target_pairs={{0,64},{1,65},{2,66},{3,67},{4,68},{5,69},{6,70},{7,71},{8,72},{9,... | collective-permute-start | bytes 1179656 | tf_op jit(solution)/shard_map/ppermute | solution.py:44
  104.3 6.6 %collective-permute-start.9 = (bf16[8,32,256]{2,1,0:T(8,128)(2,1)S(1)}, bf16[8,32,256]{2,1,0:T(8,128)(2,1)S(1)}, u32[]{:S(2)}, u32[]{:S(2)}) collective-permute-start(bf16[8,32,256]{2,1,0:T(8,128)(2,1)S(1)} %slice.8), channel_id=1, source_target_pairs={{0,128},{1,129},{2,130},{3,131},{4,132},{5,133},{6,134},{7,135},{8... | collective-permute-start | bytes 393224 | tf_op jit(solution)/shard_map/ppermute | solution.py:44
  110.9 3.1 %collective-permute-start.10 = (bf16[8,32,256]{2,1,0:T(8,128)(2,1)S(1)}, bf16[8,32,256]{2,1,0:T(8,128)(2,1)S(1)}, u32[]{:S(2)}, u32[]{:S(2)}) collective-permute-start(bf16[8,32,256]{2,1,0:T(8,128)(2,1)S(1)} %collective-permute-done.9.refs_0_), channel_id=1, source_target_pairs={{0,64},{1,65},{2,66},{3,67},{4,68},{5,69},{6,70},{7,71},{8,72},{9,... | collective-permute-start | bytes 393224 | tf_op jit(solution)/shard_map/ppermute | solution.py:44

commit v3 on v2

--- a/solution.py
+++ b/solution.py
@@ -81,7 +81,7 @@
             pltpu.make_async_copy(columns_of(src, proj, k, side), out.at[k], sem).start()
             return carry
 
-        lax.fori_loop(0, blocks, start, 0, unroll=4)
+        lax.fori_loop(0, blocks, start, 0, unroll=8)
         pltpu.make_async_copy(out, out, sem).wait()
 
     out = ((blocks, rows, WIDTH), deltas.dtype)
@@ -99,7 +99,7 @@
             out[k] = total.astype(out.dtype)
             return carry
 
-        lax.fori_loop(0, out.shape[0], body, 0, unroll=4)
+        lax.fori_loop(0, out.shape[0], body, 0, unroll=8)
 
     return on_chip(kernel, values, [(values[0].shape, values[0].dtype)])[0]
 
@@ -133,7 +133,7 @@
                 dst[k] = updated.astype(dst.dtype)
                 return carry
 
-            lax.fori_loop(0, count, body, 0, unroll=2)
+            lax.fori_loop(0, count, body, 0, unroll=4)
 
     whole, piece = (master.shape, master.dtype), (over.shape, over.dtype)
     operands = [spread, over, across, beside, master, momentum]
@@ -180,7 +180,7 @@
                 pltpu.make_async_copy(src.at[k], columns_of(out, proj, first + k, side), sems.at[j]).start()
                 return carry
 
-            lax.fori_loop(0, src.shape[0], start, 0, unroll=4)
+            lax.fori_loop(0, src.shape[0], start, 0, unroll=8)
         for j, src in enumerate(ins):
             pltpu.make_async_copy(src, src, sems.at[j]).wait()
 

time: 115 us -> 115 us (level)
  no operation moved by 1% of the time
where the time goes in v3:
time: 115 us
  blocking collectives  45.6 us (40%)
  waiting for transfers between devices  40.1 us (35%)
  starting transfers between devices  19.4 us (17%)
  Pallas kernels  8.8 us (8%)
    all_to_all x2, blocking collectives, exchange(): return lax.all_to_all(value, PLANE, split_axis=0, concat_axis=0, tiled=True)  45.6 us
    ppermute x14, waiting for transfers between devices, swap(): return lax.ppermute(value, AXES, pairs(flip))  40.1 us
    ppermute x14, starting transfers between devices, swap(): return lax.ppermute(value, AXES, pairs(flip))  19.4 us
    pallas_call x13, Pallas kernels, on_chip(): pl.pallas_call(kernel, in_specs=[FAR if k in far else NEAR for k in range...  8.8 us
  transfers between devices with their start and end apart: 14, of which 7 were waited for; matrix products, arithmetic and copies ran while one was open for 0% of the time, Pallas kernels for 6%

profile of v3, /device:TPU:1, one launch (start us, length us, event | category | flops | bytes accessed | tf_op | source)
XLA Modules:
  0.0 114.7 jit_solution(18142305796323791916)
XLA Ops:
  0.6 1.0 shard_map.61
  1.7 3.3 %collective-permute-start.1 = (bf16[32,32,256]{2,1,0:T(8,128)(2,1)S(1)}, bf16[32,32,256]{2,1,0:T(8,128)(2,1)S(1)}, u32[]{:S(2)}, u32[]{:S(2)}) collective-permute-start(bf16[32,32,256]{2,1,0:T(8,128)(2,1)S(1)} %shard_map.61), channel_id=1, source_target_pairs={{0,64},{1,65},{2,66},{3,67},{4,68},{5,69},{6,70},{7,71},{8,72},{9,... | collective-permute-start | bytes 1572872 | tf_op jit(solution)/shard_map/ppermute | solution.py:44
  5.0 1.0 shard_map.59
  6.0 0.1 collective-permute-start
  6.1 1.0 shard_map.60.refs_0_
  7.1 0.0 collective-permute-done.1.refs_1_
  7.1 0.1 shard_map.62
  7.3 1.1 collective-permute-start.2
  8.4 1.0 shard_map.58.refs_0_
  9.4 0.0 copy-start
  9.4 0.0 copy-start.1
  9.4 0.0 collective-permute-done.refs_1_
  9.5 12.4 %collective-permute-done.2.refs_2_ = bf16[32,32,256]{2,1,0:T(8,128)(2,1)S(1)} collective-permute-done((bf16[32,32,256]{2,1,0:T(8,128)(2,1)S(1)}, bf16[32,32,256]{2,1,0:T(8,128)(2,1)S(1)}, u32[]{:S(2)}, u32[]{:S(2)}) %collective-permute-start.2) | collective-permute-done | bytes 524320 | tf_op jit(solution)/shard_map/ppermute | solution.py:44
  21.9 0.2 shard_map.63
  22.1 24.7 %all_to_all.10 = bf16[32,32,256]{2,1,0:T(8,128)(2,1)S(1)} all-to-all(bf16[32,32,256]{2,1,0:T(8,128)(2,1)S(1)} %shard_map.63), channel_id=1, replica_groups=mesh['xh'=2,'c'=2,'zh'=2,'zm'=2,'z0'=2,'y'=4,'xl'=2] {'zh','zm','z0','y'}, dimensions={0} | all-to-all | bytes 1048576 | tf_op jit(solution)/shard_map/all_to_all | solution.py:48
  46.9 2.6 %collective-permute-start.3 = (bf16[8,32,256]{2,1,0:T(8,128)(2,1)S(1)}, bf16[8,32,256]{2,1,0:T(8,128)(2,1)S(1)}, u32[]{:S(2)}, u32[]{:S(2)}) collective-permute-start(bf16[8,32,256]{2,1,0:T(8,128)(2,1)S(1)} %get-tuple-element.16), channel_id=1, source_target_pairs={{0,129},{1,128},{2,131},{3,130},{4,133},{5,132},{6,135},{7,134},{8... | collective-permute-start | bytes 393224 | tf_op jit(solution)/shard_map/ppermute | solution.py:44
  49.4 3.7 %collective-permute-start.4 = (bf16[8,32,256]{2,1,0:T(8,128)(2,1)S(1)}, bf16[8,32,256]{2,1,0:T(8,128)(2,1)S(1)}, u32[]{:S(2)}, u32[]{:S(2)}) collective-permute-start(bf16[8,32,256]{2,1,0:T(8,128)(2,1)S(1)} %get-tuple-element.17), channel_id=1, source_target_pairs={{0,193},{1,192},{2,195},{3,194},{4,197},{5,196},{6,199},{7,198},{8... | collective-permute-start | bytes 393224 | tf_op jit(solution)/shard_map/ppermute | solution.py:44
  53.2 0.0 collective-permute-start.5
  53.2 0.0 collective-permute-done.3.over_ref
  53.2 5.0 %collective-permute-done.4.across_ref = bf16[8,32,256]{2,1,0:T(8,128)(2,1)S(1)} collective-permute-done((bf16[8,32,256]{2,1,0:T(8,128)(2,1)S(1)}, bf16[8,32,256]{2,1,0:T(8,128)(2,1)S(1)}, u32[]{:S(2)}, u32[]{:S(2)}) %collective-permute-start.4) | collective-permute-done | bytes 131104 | tf_op jit(solution)/shard_map/ppermute | solution.py:44
  58.1 0.0 collective-permute-done.5.beside_ref
  58.1 0.0 copy-done
  58.1 0.0 copy-done.1
  58.1 0.4 shard_map.65
  58.6 3.0 %collective-permute-start.6 = (bf16[8,32,256]{2,1,0:T(8,128)(2,1)S(1)}, bf16[8,32,256]{2,1,0:T(8,128)(2,1)S(1)}, u32[]{:S(2)}, u32[]{:S(2)}) collective-permute-start(bf16[8,32,256]{2,1,0:T(8,128)(2,1)S(1)} %get-tuple-element.24), channel_id=1, source_target_pairs={{0,129},{1,128},{2,131},{3,130},{4,133},{5,132},{6,135},{7,134},{8... | collective-permute-start | bytes 393224 | tf_op jit(solution)/shard_map/ppermute | solution.py:44
  61.5 1.1 %collective-permute-start.7 = (bf16[8,32,256]{2,1,0:T(8,128)(2,1)S(1)}, bf16[8,32,256]{2,1,0:T(8,128)(2,1)S(1)}, u32[]{:S(2)}, u32[]{:S(2)}) collective-permute-start(bf16[8,32,256]{2,1,0:T(8,128)(2,1)S(1)} %get-tuple-element.25), channel_id=1, source_target_pairs={{0,193},{1,192},{2,195},{3,194},{4,197},{5,196},{6,199},{7,198},{8... | collective-permute-start | bytes 393224 | tf_op jit(solution)/shard_map/ppermute | solution.py:44
  62.7 0.0 collective-permute-start.8
  62.7 2.2 %collective-permute-done.6.over_ref = bf16[8,32,256]{2,1,0:T(8,128)(2,1)S(1)} collective-permute-done((bf16[8,32,256]{2,1,0:T(8,128)(2,1)S(1)}, bf16[8,32,256]{2,1,0:T(8,128)(2,1)S(1)}, u32[]{:S(2)}, u32[]{:S(2)}) %collective-permute-start.6) | collective-permute-done | bytes 131104 | tf_op jit(solution)/shard_map/ppermute | solution.py:44
  64.8 3.3 %collective-permute-done.7.across_ref = bf16[8,32,256]{2,1,0:T(8,128)(2,1)S(1)} collective-permute-done((bf16[8,32,256]{2,1,0:T(8,128)(2,1)S(1)}, bf16[8,32,256]{2,1,0:T(8,128)(2,1)S(1)}, u32[]{:S(2)}, u32[]{:S(2)}) %collective-permute-start.7) | collective-permute-done | bytes 131104 | tf_op jit(solution)/shard_map/ppermute | solution.py:44
  68.1 0.0 collective-permute-done.8.beside_ref
  68.2 20.8 %all_to_all.11.refs_0_ = bf16[32,32,256]{2,1,0:T(8,128)(2,1)S(1)} all-to-all(bf16[32,32,256]{2,1,0:T(8,128)(2,1)S(1)} %bitcast.5), channel_id=1, replica_groups=mesh['xh'=2,'c'=2,'zh'=2,'zm'=2,'z0'=2,'y'=4,'xl'=2] {'zh','zm','z0','y'}, dimensions={0} | all-to-all | bytes 1048576 | tf_op jit(solution)/shard_map/all_to_all | solution.py:48
  89.0 2.1 %collective-permute-start.12 = (bf16[32,32,256]{2,1,0:T(8,128)(2,1)S(1)}, bf16[32,32,256]{2,1,0:T(8,128)(2,1)S(1)}, u32[]{:S(2)}, u32[]{:S(2)}) collective-permute-start(bf16[32,32,256]{2,1,0:T(8,128)(2,1)S(1)} %all_to_all.11.refs_0_), channel_id=1, source_target_pairs={{0,64},{1,65},{2,66},{3,67},{4,68},{5,69},{6,70},{7,71},{8,72},{9,... | collective-permute-start | bytes 1572872 | tf_op jit(solution)/shard_map/ppermute | solution.py:44
  91.1 0.4 collective-permute-start.11
  91.5 1.1 collective-permute-done.12.refs_1_
  92.6 1.0 shard_map.68.refs_2_
  93.6 9.8 %collective-permute-done.11.refs_0_ = bf16[24,32,256]{2,1,0:T(8,128)(2,1)S(1)} collective-permute-done((bf16[24,32,256]{2,1,0:T(8,128)(2,1)S(1)}, bf16[24,32,256]{2,1,0:T(8,128)(2,1)S(1)}, u32[]{:S(2)}, u32[]{:S(2)}) %collective-permute-start.11) | collective-permute-done | bytes 393248 | tf_op jit(solution)/shard_map/ppermute | solution.py:44
  103.4 0.9 collective-permute-start.13
  104.2 0.4 collective-permute-start.9
  104.6 6.3 %collective-permute-done.9.refs_0_ = bf16[8,32,256]{2,1,0:T(8,128)(2,1)S(1)} collective-permute-done((bf16[8,32,256]{2,1,0:T(8,128)(2,1)S(1)}, bf16[8,32,256]{2,1,0:T(8,128)(2,1)S(1)}, u32[]{:S(2)}, u32[]{:S(2)}) %collective-permute-start.9) | collective-permute-done | bytes 131104 | tf_op jit(solution)/shard_map/ppermute | solution.py:44
  110.9 0.9 collective-permute-start.10
  111.7 1.3 %shard_map.66 = (f32[2,512,256]{2,1,0:T(8,128)}, f32[2,512,256]{2,1,0:T(8,128)}) custom-call(f32[2,512,256]{2,1,0:T(8,128)S(1)} %get-tuple-element.19.first_ref, f32[2,512,256]{2,1,0:T(8,128)S(1)} %get-tuple-element.20.second_ref), custom_call_target="tpu_custom_call" | custom-call | tf_op jit(solution)/shard_map/pallas_call | solution.py:55
  113.1 0.0 collective-permute-done.13.refs_1_
  113.1 0.9 shard_map.69.refs_2_
  114.0 0.0 collective-permute-done.10.refs_1_
  114.0 0.7 shard_map.70
  (4 shorter events, 0.1 us)
Async XLA Ops:
  1.7 5.5 %collective-permute-start.1 = (bf16[32,32,256]{2,1,0:T(8,128)(2,1)S(1)}, bf16[32,32,256]{2,1,0:T(8,128)(2,1)S(1)}, u32[]{:S(2)}, u32[]{:S(2)}) collective-permute-start(bf16[32,32,256]{2,1,0:T(8,128)(2,1)S(1)} %shard_map.61), channel_id=1, source_target_pairs={{0,64},{1,65},{2,66},{3,67},{4,68},{5,69},{6,70},{7,71},{8,72},{9,... | collective-permute-start | bytes 1572872 | tf_op jit(solution)/shard_map/ppermute | solution.py:44
  6.0 3.5 %collective-permute-start = (bf16[32,32,256]{2,1,0:T(8,128)(2,1)S(1)}, bf16[32,32,256]{2,1,0:T(8,128)(2,1)S(1)}, u32[]{:S(2)}, u32[]{:S(2)}) collective-permute-start(bf16[32,32,256]{2,1,0:T(8,128)(2,1)S(1)} %shard_map.59), channel_id=1, source_target_pairs={{0,64},{1,65},{2,66},{3,67},{4,68},{5,69},{6,70},{7,71},{8,72},{9,... | collective-permute-start | bytes 1572872 | tf_op jit(solution)/shard_map/ppermute | solution.py:44
  7.3 14.6 %collective-permute-start.2 = (bf16[32,32,256]{2,1,0:T(8,128)(2,1)S(1)}, bf16[32,32,256]{2,1,0:T(8,128)(2,1)S(1)}, u32[]{:S(2)}, u32[]{:S(2)}) collective-permute-start(bf16[32,32,256]{2,1,0:T(8,128)(2,1)S(1)} %shard_map.62), channel_id=1, source_target_pairs={{0,128},{1,129},{2,130},{3,131},{4,132},{5,133},{6,134},{7,135},{8... | collective-permute-start | bytes 1572872 | tf_op jit(solution)/shard_map/ppermute | solution.py:44
  9.4 48.7 %copy-start = (f32[2,512,256]{2,1,0:T(8,128)S(1)}, f32[2,512,256]{2,1,0:T(8,128)}, u32[]{:S(2)}) copy-start(f32[2,512,256]{2,1,0:T(8,128)} %m_ref.1) | copy-start | bytes 3145732
  9.4 48.7 %copy-start.1 = (f32[2,512,256]{2,1,0:T(8,128)S(1)}, f32[2,512,256]{2,1,0:T(8,128)}, u32[]{:S(2)}) copy-start(f32[2,512,256]{2,1,0:T(8,128)} %v_ref.1) | copy-start | bytes 3145732
  46.9 6.3 %collective-permute-start.3 = (bf16[8,32,256]{2,1,0:T(8,128)(2,1)S(1)}, bf16[8,32,256]{2,1,0:T(8,128)(2,1)S(1)}, u32[]{:S(2)}, u32[]{:S(2)}) collective-permute-start(bf16[8,32,256]{2,1,0:T(8,128)(2,1)S(1)} %get-tuple-element.16), channel_id=1, source_target_pairs={{0,129},{1,128},{2,131},{3,130},{4,133},{5,132},{6,135},{7,134},{8... | collective-permute-start | bytes 393224 | tf_op jit(solution)/shard_map/ppermute | solution.py:44
  49.4 8.7 %collective-permute-start.4 = (bf16[8,32,256]{2,1,0:T(8,128)(2,1)S(1)}, bf16[8,32,256]{2,1,0:T(8,128)(2,1)S(1)}, u32[]{:S(2)}, u32[]{:S(2)}) collective-permute-start(bf16[8,32,256]{2,1,0:T(8,128)(2,1)S(1)} %get-tuple-element.17), channel_id=1, source_target_pairs={{0,193},{1,192},{2,195},{3,194},{4,197},{5,196},{6,199},{7,198},{8... | collective-permute-start | bytes 393224 | tf_op jit(solution)/shard_map/ppermute | solution.py:44
  53.2 5.0 %collective-permute-start.5 = (bf16[8,32,256]{2,1,0:T(8,128)(2,1)S(1)}, bf16[8,32,256]{2,1,0:T(8,128)(2,1)S(1)}, u32[]{:S(2)}, u32[]{:S(2)}) collective-permute-start(bf16[8,32,256]{2,1,0:T(8,128)(2,1)S(1)} %get-tuple-element.18), channel_id=1, source_target_pairs={{0,64},{1,65},{2,66},{3,67},{4,68},{5,69},{6,70},{7,71},{8,72},{9,... | collective-permute-start | bytes 393224 | tf_op jit(solution)/shard_map/ppermute | solution.py:44
  58.6 6.3 %collective-permute-start.6 = (bf16[8,32,256]{2,1,0:T(8,128)(2,1)S(1)}, bf16[8,32,256]{2,1,0:T(8,128)(2,1)S(1)}, u32[]{:S(2)}, u32[]{:S(2)}) collective-permute-start(bf16[8,32,256]{2,1,0:T(8,128)(2,1)S(1)} %get-tuple-element.24), channel_id=1, source_target_pairs={{0,129},{1,128},{2,131},{3,130},{4,133},{5,132},{6,135},{7,134},{8... | collective-permute-start | bytes 393224 | tf_op jit(solution)/shard_map/ppermute | solution.py:44
  61.5 6.6 %collective-permute-start.7 = (bf16[8,32,256]{2,1,0:T(8,128)(2,1)S(1)}, bf16[8,32,256]{2,1,0:T(8,128)(2,1)S(1)}, u32[]{:S(2)}, u32[]{:S(2)}) collective-permute-start(bf16[8,32,256]{2,1,0:T(8,128)(2,1)S(1)} %get-tuple-element.25), channel_id=1, source_target_pairs={{0,193},{1,192},{2,195},{3,194},{4,197},{5,196},{6,199},{7,198},{8... | collective-permute-start | bytes 393224 | tf_op jit(solution)/shard_map/ppermute | solution.py:44
  62.7 5.5 %collective-permute-start.8 = (bf16[8,32,256]{2,1,0:T(8,128)(2,1)S(1)}, bf16[8,32,256]{2,1,0:T(8,128)(2,1)S(1)}, u32[]{:S(2)}, u32[]{:S(2)}) collective-permute-start(bf16[8,32,256]{2,1,0:T(8,128)(2,1)S(1)} %get-tuple-element.26), channel_id=1, source_target_pairs={{0,64},{1,65},{2,66},{3,67},{4,68},{5,69},{6,70},{7,71},{8,72},{9,... | collective-permute-start | bytes 393224 | tf_op jit(solution)/shard_map/ppermute | solution.py:44
  89.0 3.6 %collective-permute-start.12 = (bf16[32,32,256]{2,1,0:T(8,128)(2,1)S(1)}, bf16[32,32,256]{2,1,0:T(8,128)(2,1)S(1)}, u32[]{:S(2)}, u32[]{:S(2)}) collective-permute-start(bf16[32,32,256]{2,1,0:T(8,128)(2,1)S(1)} %all_to_all.11.refs_0_), channel_id=1, source_target_pairs={{0,64},{1,65},{2,66},{3,67},{4,68},{5,69},{6,70},{7,71},{8,72},{9,... | collective-permute-start | bytes 1572872 | tf_op jit(solution)/shard_map/ppermute | solution.py:44
  91.1 12.3 %collective-permute-start.11 = (bf16[24,32,256]{2,1,0:T(8,128)(2,1)S(1)}, bf16[24,32,256]{2,1,0:T(8,128)(2,1)S(1)}, u32[]{:S(2)}, u32[]{:S(2)}) collective-permute-start(bf16[24,32,256]{2,1,0:T(8,128)(2,1)S(1)} %slice.9), channel_id=1, source_target_pairs={{0,128},{1,129},{2,130},{3,131},{4,132},{5,133},{6,134},{7,135},{8... | collective-permute-start | bytes 1179656 | tf_op jit(solution)/shard_map/ppermute | solution.py:44
  103.4 9.7 %collective-permute-start.13 = (bf16[24,32,256]{2,1,0:T(8,128)(2,1)S(1)}, bf16[24,32,256]{2,1,0:T(8,128)(2,1)S(1)}, u32[]{:S(2)}, u32[]{:S(2)}) collective-permute-start(bf16[24,32,256]{2,1,0:T(8,128)(2,1)S(1)} %collective-permute-done.11.refs_0_), channel_id=1, source_target_pairs={{0,64},{1,65},{2,66},{3,67},{4,68},{5,69},{6,70},{7,71},{8,72},{9,... | collective-permute-start | bytes 1179656 | tf_op jit(solution)/shard_map/ppermute | solution.py:44
  104.2 6.6 %collective-permute-start.9 = (bf16[8,32,256]{2,1,0:T(8,128)(2,1)S(1)}, bf16[8,32,256]{2,1,0:T(8,128)(2,1)S(1)}, u32[]{:S(2)}, u32[]{:S(2)}) collective-permute-start(bf16[8,32,256]{2,1,0:T(8,128)(2,1)S(1)} %slice.8), channel_id=1, source_target_pairs={{0,128},{1,129},{2,130},{3,131},{4,132},{5,133},{6,134},{7,135},{8... | collective-permute-start | bytes 393224 | tf_op jit(solution)/shard_map/ppermute | solution.py:44
  110.9 3.1 %collective-permute-start.10 = (bf16[8,32,256]{2,1,0:T(8,128)(2,1)S(1)}, bf16[8,32,256]{2,1,0:T(8,128)(2,1)S(1)}, u32[]{:S(2)}, u32[]{:S(2)}) collective-permute-start(bf16[8,32,256]{2,1,0:T(8,128)(2,1)S(1)} %collective-permute-done.9.refs_0_), channel_id=1, source_target_pairs={{0,64},{1,65},{2,66},{3,67},{4,68},{5,69},{6,70},{7,71},{8,72},{9,... | collective-permute-start | bytes 393224 | tf_op jit(solution)/shard_map/ppermute | solution.py:44
